TPU v7x, 32 devices: a whole 2x2x4 slice. The times are simulated.
32 devices in a mesh: dp: 4 (over y, core), row: 2 (over x), col: 4 (over z).
Axes of the slice: x: 2, y: 2, z: 4, core: 2. Of those that a mesh axis runs over, the one named last changes fastest.
Arguments:
- tokens: bfloat16 [2048, 1024], P(('dp', 'row'), 'col'), may hold values from -6 to 6
- segment_index: int32 [4, 512], P('dp'), may hold values from 0 to 1, as said below
- cotangent: bfloat16 [2048, 1024], P(('dp', 'row'), 'col'), may hold values from -6 to 6
- norm_gain: float32 [2, 1024], P(None, 'col'), may hold values from 0.25 to 1.75
- gate_weight: bfloat16 [2, 1024, 2048], P(None, 'row', 'col'), may hold values from -0.1875 to 0.1875
- inner_weight: bfloat16 [2, 1024, 2048], P(None, 'row', 'col'), may hold values from -0.1875 to 0.1875
- state_weight: bfloat16 [2, 1024, 256], P(None, 'row'), may hold values from -0.1875 to 0.1875
- step_weight: bfloat16 [2, 1024, 32], P(None, 'row', 'col'), may hold values from -0.1875 to 0.1875
- inner_kernel: float32 [2, 2048, 4], P(None, 'col'), may hold values from -3 to 3
- inner_bias: float32 [2, 2048], P(None, 'col'), may hold values from -0.5 to 0.5
- state_kernel: float32 [2, 256, 4], replicated, may hold values from -3 to 3
- state_bias: float32 [2, 256], replicated, may hold values from -0.5 to 0.5
- step_bias: float32 [2, 32], P(None, 'col'), may hold values from -4 to -1
- decay_log: float32 [2, 32], P(None, 'col'), may hold values from -6.5 to 0.5
- skip_gain: float32 [2, 32], P(None, 'col'), may hold values from 0.5 to 1.5
- gated_gain: float32 [2, 2048], P(None, 'col'), may hold values from 0.25 to 1.75
- output_weight: bfloat16 [2, 2048, 1024], P(None, 'col', 'row'), may hold values from -0.125 to 0.125
Outputs:
- layer_output: bfloat16 [2048, 1024], P(('dp', 'row'), 'col')
- input_grad: float32 [2048, 1024], P(('dp', 'row'), 'col')
- norm_gain_grad: float32 [2, 1024], P(None, 'col')
- gate_weight_grad: float32 [2, 1024, 2048], P(None, ('dp', 'row'), 'col')
- inner_weight_grad: float32 [2, 1024, 2048], P(None, ('dp', 'row'), 'col')
- state_weight_grad: float32 [2, 1024, 256], P(None, ('dp', 'row'), 'col')
- step_weight_grad: float32 [2, 1024, 32], P(None, ('dp', 'row'), 'col')
- inner_kernel_grad: float32 [2, 2048, 4], P(None, 'col')
- inner_bias_grad: float32 [2, 2048], P(None, 'col')
- state_kernel_grad: float32 [2, 256, 4], P(None, 'col')
- state_bias_grad: float32 [2, 256], P(None, 'col')
- step_bias_grad: float32 [2, 32], P(None, 'col')
- decay_log_grad: float32 [2, 32], P(None, 'col')
- skip_gain_grad: float32 [2, 32], P(None, 'col')
- gated_gain_grad: float32 [2, 2048], P(None, 'col')
- output_weight_grad: float32 [2, 2048, 1024], P(None, 'col', ('dp', 'row'))
Inputs may be any that keep to these rules, and one draw needn't show every extreme that they name: `segment_index`: each row is one group of 512 tokens holding two sequences: 0 up to a boundary, 1 from it on; each sequence has at least 2048 tokens, or a quarter of 512 where that is fewer.
All inputs are finite; a program needn't handle non-finite values.
Results may differ from a plain program's by a relative error of at most 0.0085.
The roundings to bfloat16 on the way count: a program that leaves them out, or rounds other values in their place, can miss the bound.
Values may be sent and summed in bfloat16 or wider, within the bound.
A program may use at most 128 MiB of HBM per device.

v0:
```python
import jax
import jax.numpy as jnp
from jax import lax
from jax.sharding import PartitionSpec as P

KERNEL = 4
SPAN = 256
LAYERS = 2


EPSILON = 1e-05
HIGHEST = lax.Precision.HIGHEST


def passed_along(value, axis, by):
    devices = lax.axis_size(axis)
    pairs = [(i, i + by) for i in range(devices) if 0 <= i + by < devices]
    return lax.ppermute(value, axis, pairs)


def carried_in(part, axis, combine, identity, reverse):
    count = lax.axis_size(axis)
    place = lax.axis_index(axis)
    ahead = count - 1 - place if reverse else place
    gathered = jax.tree.map(lambda a: lax.all_gather(a, axis), part)
    state = jax.tree.map(lambda a, e: jnp.zeros_like(a) + jnp.asarray(e, a.dtype), part, identity)

    def one(turn, state):
        source = count - 1 - turn if reverse else turn
        return combine(
            state, jax.tree.map(lambda a: lax.dynamic_index_in_dim(a, source, 0, False), gathered)
        )

    return lax.fori_loop(0, ahead, one, state)


def row_total(values):
    return lax.psum(values, "col")


def link_up(earlier, later):
    return (earlier[0] * later[0], later[0][:, None, None] * earlier[1] + later[1])


def link_down(earlier, later):
    return (earlier[0] * later[0], later[1] + later[0][:, None, None] * earlier[1])


def mixer_parts(
    post_x, b_mat, c_mat, raw_step, step_off, decay_rate, skip_rate, segments, seg_prior
):
    tok_count = post_x.shape[0]
    head_count = raw_step.shape[1]
    head_width = post_x.shape[1] // head_count
    block_count = tok_count // SPAN
    step_size = jax.nn.softplus(raw_step + step_off[None, :])
    decay_now = -jnp.exp(decay_rate)[None, :] * step_size
    xs_c = post_x.reshape(block_count, SPAN, head_count, head_width)
    step_c = step_size.reshape(block_count, SPAN, head_count)
    cumulative = jnp.cumsum(decay_now.reshape(block_count, SPAN, head_count), axis=1)
    b_c = b_mat.reshape(block_count, SPAN, -1)
    c_c = c_mat.reshape(block_count, SPAN, -1)
    seg_c = segments.reshape(block_count, SPAN)
    places = jnp.arange(SPAN)
    same_seq = (seg_c[:, :, None] == seg_c[:, None, :]) & (places[:, None] >= places[None, :])[None]
    causal = same_seq.astype(jnp.float32)[:, None, :, :]
    cum_heads = jnp.transpose(cumulative, (0, 2, 1))
    step_heads = jnp.transpose(step_c, (0, 2, 1))
    spread = cum_heads[:, :, :, None] - cum_heads[:, :, None, :]
    scores = jnp.einsum("cin,cjn->cij", c_c, b_c, precision=HIGHEST)
    weights = jnp.exp(spread * causal) * causal * scores[:, None, :, :] * step_heads[:, :, None, :]
    intra_part = jnp.einsum("chij,cjhp->cihp", weights, xs_c, precision=HIGHEST)
    entry_gate = jnp.exp(cumulative) * (seg_c == seg_prior[:, None]).astype(jnp.float32)[..., None]
    tail_gate = (
        jnp.exp(cumulative[:, -1:, :] - cumulative)
        * (seg_c == seg_c[:, -1:]).astype(jnp.float32)[..., None]
        * step_c
    )
    fresh_state = jnp.einsum("cjh,cjhp,cjn->chpn", tail_gate, xs_c, b_c, precision=HIGHEST)
    block_decay = (
        jnp.exp(cumulative[:, -1, :]) * (seg_c[:, -1] == seg_prior).astype(jnp.float32)[:, None]
    )

    def advance(state_now, element):
        return (element[1][:, None, None] * state_now + element[0], state_now)

    dev_state, starts = lax.scan(
        advance, jnp.zeros_like(fresh_state[0]), (fresh_state, block_decay)
    )
    prefix = jnp.cumprod(
        jnp.concatenate([jnp.ones_like(block_decay), block_decay[:-1]], axis=0), axis=0
    )
    dev_decay = prefix[-1] * block_decay[-1]
    local_part = intra_part + skip_rate[None, None, :, None] * xs_c
    return (local_part, entry_gate, c_c, starts, prefix, dev_state, dev_decay)


def mixer_finish(pieces, entry_state):
    local_part, entry_gate, c_c, starts, prefix, dev_state, dev_decay = pieces
    states = starts + prefix[:, :, None, None] * entry_state[None]
    incoming = jnp.einsum("chpn,cin->cihp", states, c_c, precision=HIGHEST)
    mixed_out = local_part + entry_gate[..., None] * incoming
    return mixed_out.reshape(mixed_out.shape[0] * SPAN, -1)


def mixer_core(
    post_x,
    b_mat,
    c_mat,
    raw_step,
    step_off,
    decay_rate,
    skip_rate,
    entry_state,
    segments,
    seg_prior,
):
    pieces = mixer_parts(
        post_x, b_mat, c_mat, raw_step, step_off, decay_rate, skip_rate, segments, seg_prior
    )
    return (mixer_finish(pieces, entry_state), pieces[5], pieces[6])


def local(
    tokens,
    segment_index,
    cotangent,
    norm_gain,
    gate_weight,
    inner_weight,
    state_weight,
    step_weight,
    inner_kernel,
    inner_bias,
    state_kernel,
    state_bias,
    step_bias,
    decay_log,
    skip_gain,
    gated_gain,
    output_weight,
):
    tok_rows = tokens.shape[0]
    full_width = tokens.shape[1] * lax.axis_size("col")
    head_count = step_bias.shape[1]
    inner_cols = inner_kernel.shape[1]
    inner_full = inner_cols * lax.axis_size("col")
    state_cols = state_kernel.shape[1]
    state_half = state_cols // 2
    share_cols = state_cols // lax.axis_size("col")
    col_at = lax.axis_index("col")
    first_tok = lax.axis_index("row") * tok_rows
    group_seg = segment_index[0]
    seg_front = jnp.concatenate([jnp.full((KERNEL - 1,), -1, jnp.int32), group_seg])
    seg_rear = jnp.concatenate([group_seg, jnp.full((KERNEL - 1,), -2, jnp.int32)])
    seg_early = lax.dynamic_slice_in_dim(seg_front, first_tok, tok_rows + KERNEL - 1)
    seg_late = lax.dynamic_slice_in_dim(seg_rear, first_tok, tok_rows + KERNEL - 1)
    segments = seg_early[KERNEL - 1 :]
    seg_prior = jnp.concatenate(
        [seg_early[KERNEL - 2 : KERNEL - 1], segments[SPAN - 1 : -1 : SPAN]]
    )
    dims_t = (((1,), (1,)), ((), ()))
    dims_w = (((0,), (0,)), ((), ()))
    resid = tokens.astype(jnp.float32)
    saved = []
    for layer_at in range(LAYERS):
        gathered = (
            lax.all_gather(gate_weight[layer_at], "row", axis=0, tiled=True),
            lax.all_gather(inner_weight[layer_at], "row", axis=0, tiled=True),
            lax.all_gather(state_weight[layer_at], "row", axis=0, tiled=True),
            lax.all_gather(step_weight[layer_at], "row", axis=0, tiled=True),
            lax.all_gather(output_weight[layer_at], "row", axis=1, tiled=True),
        )
        gate_full, inner_whole, state_full, step_full, output_full = gathered
        square = row_total(jnp.sum(resid * resid, axis=1))
        row_scale = lax.rsqrt(square / full_width + EPSILON)
        normed = (resid * row_scale[:, None] * norm_gain[layer_at][None, :]).astype(jnp.bfloat16)
        normed_all = lax.all_gather(normed, "col", axis=1, tiled=True)
        gate_val = jnp.dot(normed_all, gate_full, preferred_element_type=jnp.float32)
        inner_val = jnp.dot(normed_all, inner_whole, preferred_element_type=jnp.float32)
        pair_val = jnp.dot(normed_all, state_full, preferred_element_type=jnp.float32)
        raw_step = jnp.dot(normed_all, step_full, preferred_element_type=jnp.float32)
        values = jnp.concatenate([inner_val, pair_val], axis=1)
        before = passed_along(values[tok_rows - (KERNEL - 1) :], "row", 1)
        padded = jnp.concatenate([before, values], axis=0)
        kernels = jnp.concatenate([inner_kernel[layer_at], state_kernel[layer_at]], axis=0)
        pre_act = (
            jnp.zeros_like(values)
            + jnp.concatenate([inner_bias[layer_at], state_bias[layer_at]])[None, :]
        )
        for offset in range(KERNEL):
            same_seq = (seg_early[offset : offset + tok_rows] == segments).astype(jnp.float32)
            pre_act = (
                pre_act
                + kernels[:, offset][None, :]
                * padded[offset : offset + tok_rows]
                * same_seq[:, None]
            )
        post_act = jax.nn.silu(pre_act)
        post_x = post_act[:, :inner_cols]
        b_mat = post_act[:, inner_cols : inner_cols + state_half]
        c_mat = post_act[:, inner_cols + state_half :]
        pieces = mixer_parts(
            post_x,
            b_mat,
            c_mat,
            raw_step,
            step_bias[layer_at],
            decay_log[layer_at],
            skip_gain[layer_at],
            segments,
            seg_prior,
        )
        unused, entry_state = carried_in(
            (pieces[6], pieces[5]),
            "row",
            link_up,
            (jnp.ones_like(pieces[6]), jnp.zeros_like(pieces[5])),
            False,
        )
        mixed_out = mixer_finish(pieces, entry_state)
        silu_gate = jax.nn.silu(gate_val)
        gated = mixed_out * silu_gate
        power_sum = row_total(jnp.sum(gated * gated, axis=1))
        gated_scale = lax.rsqrt(power_sum / inner_full + EPSILON)
        normed_y = (gated * gated_scale[:, None] * gated_gain[layer_at][None, :]).astype(
            jnp.bfloat16
        )
        partial_out = jnp.dot(normed_y, output_full, preferred_element_type=jnp.float32)
        branch = lax.psum_scatter(partial_out, "col", scatter_dimension=1, tiled=True)
        stored = None
        saved.append(
            (
                resid,
                row_scale,
                normed_all,
                gate_val,
                padded,
                pre_act,
                post_x,
                b_mat,
                c_mat,
                raw_step,
                entry_state,
                pieces[4],
                pieces[1],
                pieces[6],
                mixed_out,
                silu_gate,
                gated,
                gated_scale,
                normed_y,
                stored,
            )
        )
        resid = resid + branch
    layer_output = resid.astype(jnp.bfloat16)
    resid_grad = cotangent.astype(jnp.float32)
    grads_gate, grads_inner, grads_pair, grads_step, grads_out = ([], [], [], [], [])
    small_terms = []
    for layer_at in reversed(range(LAYERS)):
        (
            resid,
            row_scale,
            normed_all,
            gate_val,
            padded,
            pre_act,
            post_x,
            b_mat,
            c_mat,
            raw_step,
            entry_state,
            prefix,
            entry_gate,
            dev_decay,
            mixed_out,
            silu_gate,
            gated,
            gated_scale,
            normed_y,
            stored,
        ) = saved[layer_at]
        gate_full, inner_whole, state_full, step_full, output_full = (
            lax.all_gather(gate_weight[layer_at], "row", axis=0, tiled=True),
            lax.all_gather(inner_weight[layer_at], "row", axis=0, tiled=True),
            lax.all_gather(state_weight[layer_at], "row", axis=0, tiled=True),
            lax.all_gather(step_weight[layer_at], "row", axis=0, tiled=True),
            lax.all_gather(output_weight[layer_at], "row", axis=1, tiled=True),
        )
        cot_low = resid_grad.astype(jnp.bfloat16)
        cot_all = lax.all_gather(cot_low, "col", axis=1, tiled=True)
        d_normed_y = lax.dot_general(
            cot_all, output_full, dims_t, preferred_element_type=jnp.float32
        )
        grads_out.append(
            lax.dot_general(cot_all, normed_y, dims_w, preferred_element_type=jnp.float32)
        )
        scaled_y = d_normed_y * gated_gain[layer_at][None, :]
        total_y = row_total(jnp.sum(scaled_y * gated, axis=1))
        d_gated = (
            gated_scale[:, None] * scaled_y
            - gated * (gated_scale**3 * total_y / inner_full)[:, None]
        )
        gain_y = jnp.sum(d_normed_y * gated * gated_scale[:, None], axis=0)
        d_mixed = d_gated * silu_gate
        sigma_gate = jax.nn.sigmoid(gate_val)
        d_gate = d_gated * mixed_out * sigma_gate * (1.0 + gate_val * (1.0 - sigma_gate))
        block_count = tok_rows // SPAN
        d_mixed_c = d_mixed.reshape(block_count, SPAN, head_count, -1)
        c_blocks = c_mat.reshape(block_count, SPAN, -1)
        reach_gate = prefix[:, None, :] * entry_gate
        local_pull = jnp.einsum(
            "cih,cihp,cin->hpn", reach_gate, d_mixed_c, c_blocks, precision=HIGHEST
        )
        unused_b, state_pull = carried_in(
            (dev_decay, local_pull),
            "row",
            link_down,
            (jnp.ones_like(dev_decay), jnp.zeros_like(local_pull)),
            True,
        )
        decay_pull = jnp.sum(state_pull * entry_state, axis=(1, 2))

        def local_mixer(px_val, bm_val, cm_val, rs_val, so_val, dr_val, sr_val, es_val):
            return mixer_core(
                px_val, bm_val, cm_val, rs_val, so_val, dr_val, sr_val, es_val, segments, seg_prior
            )

        unused_c, pullback = jax.vjp(
            local_mixer,
            post_x,
            b_mat,
            c_mat,
            raw_step,
            step_bias[layer_at],
            decay_log[layer_at],
            skip_gain[layer_at],
            entry_state,
        )
        d_post_x, grad_b, grad_c, d_raw_step, g_step_bias, g_decay, g_skip, unused_d = pullback(
            (d_mixed, state_pull, decay_pull)
        )
        d_share = lax.psum_scatter(
            jnp.concatenate([grad_b, grad_c], axis=1), "col", scatter_dimension=1, tiled=True
        )
        d_post = jnp.concatenate([d_post_x, d_share], axis=1)
        share_pre = lax.dynamic_slice_in_dim(
            pre_act[:, inner_cols:], col_at * share_cols, share_cols, 1
        )
        own_pre = jnp.concatenate([pre_act[:, :inner_cols], share_pre], axis=1)
        sigma_pre = jax.nn.sigmoid(own_pre)
        d_pre = d_post * sigma_pre * (1.0 + own_pre * (1.0 - sigma_pre))
        after_rows = passed_along(d_pre[: KERNEL - 1], "row", -1)
        d_pre_ext = jnp.concatenate([d_pre, after_rows], axis=0)
        share_kernel = lax.dynamic_slice_in_dim(
            state_kernel[layer_at], col_at * share_cols, share_cols, 0
        )
        own_kernel = jnp.concatenate([inner_kernel[layer_at], share_kernel], axis=0)
        share_padded = lax.dynamic_slice_in_dim(
            padded[:, inner_cols:], col_at * share_cols, share_cols, 1
        )
        own_padded = jnp.concatenate([padded[:, :inner_cols], share_padded], axis=1)
        d_values = jnp.zeros_like(d_pre)
        kernel_terms = []
        for offset in range(KERNEL):
            lead_by = KERNEL - 1 - offset
            same_back = (seg_late[lead_by : lead_by + tok_rows] == segments).astype(jnp.float32)
            d_values = (
                d_values
                + own_kernel[:, offset][None, :]
                * d_pre_ext[lead_by : lead_by + tok_rows]
                * same_back[:, None]
            )
            same_fwd = (seg_early[offset : offset + tok_rows] == segments).astype(jnp.float32)
            kernel_terms.append(
                jnp.sum(d_pre * own_padded[offset : offset + tok_rows] * same_fwd[:, None], axis=0)
            )
        kernel_grad = jnp.stack(kernel_terms, axis=1)
        bias_grad = jnp.sum(d_pre, axis=0)
        d_gate16 = d_gate.astype(jnp.bfloat16)
        d_inner16 = d_values[:, :inner_cols].astype(jnp.bfloat16)
        d_pair16 = d_values[:, inner_cols:].astype(jnp.bfloat16)
        d_step16 = d_raw_step.astype(jnp.bfloat16)
        share_weight = lax.dynamic_slice_in_dim(state_full, col_at * share_cols, share_cols, 1)
        partial_in = lax.dot_general(
            d_gate16, gate_full, dims_t, preferred_element_type=jnp.float32
        )
        partial_in = partial_in + lax.dot_general(
            d_inner16, inner_whole, dims_t, preferred_element_type=jnp.float32
        )
        partial_in = partial_in + lax.dot_general(
            d_pair16, share_weight, dims_t, preferred_element_type=jnp.float32
        )
        partial_in = partial_in + lax.dot_general(
            d_step16, step_full, dims_t, preferred_element_type=jnp.float32
        )
        d_normed = lax.psum_scatter(partial_in, "col", scatter_dimension=1, tiled=True)
        grads_gate.append(
            lax.dot_general(normed_all, d_gate16, dims_w, preferred_element_type=jnp.float32)
        )
        grads_inner.append(
            lax.dot_general(normed_all, d_inner16, dims_w, preferred_element_type=jnp.float32)
        )
        grads_pair.append(
            lax.dot_general(normed_all, d_pair16, dims_w, preferred_element_type=jnp.float32)
        )
        grads_step.append(
            lax.dot_general(normed_all, d_step16, dims_w, preferred_element_type=jnp.float32)
        )
        scaled_in = d_normed * norm_gain[layer_at][None, :]
        total_in = row_total(jnp.sum(scaled_in * resid, axis=1))
        gain_in = jnp.sum(d_normed * resid * row_scale[:, None], axis=0)
        resid_grad = (
            resid_grad
            + row_scale[:, None] * scaled_in
            - resid * (row_scale**3 * total_in / full_width)[:, None]
        )
        small_terms.append(
            (
                gain_in,
                gain_y,
                kernel_grad[:inner_cols],
                bias_grad[:inner_cols],
                kernel_grad[inner_cols:],
                bias_grad[inner_cols:],
                g_step_bias,
                g_decay,
                g_skip,
            )
        )

    def stacked(items):
        return jnp.stack(items[::-1], axis=0)

    def column(slot):
        return jnp.stack([terms[slot] for terms in small_terms[::-1]], axis=0)

    summed = (
        lax.psum_scatter(stacked(grads_gate), ("dp", "row"), scatter_dimension=1, tiled=True),
        lax.psum_scatter(stacked(grads_inner), ("dp", "row"), scatter_dimension=1, tiled=True),
        lax.psum_scatter(stacked(grads_pair), ("dp", "row"), scatter_dimension=1, tiled=True),
        lax.psum_scatter(stacked(grads_step), ("dp", "row"), scatter_dimension=1, tiled=True),
        lax.psum_scatter(stacked(grads_out), ("dp", "row"), scatter_dimension=1, tiled=True),
    )
    smalls = lax.psum(
        (
            column(0),
            column(1),
            column(2),
            column(3),
            column(4),
            column(5),
            column(6),
            column(7),
            column(8),
        ),
        ("dp", "row"),
    )
    return (
        layer_output,
        resid_grad,
        smalls[0],
        summed[0],
        summed[1],
        summed[2],
        summed[3],
        smalls[2],
        smalls[3],
        smalls[4],
        smalls[5],
        smalls[6],
        smalls[7],
        smalls[8],
        smalls[1],
        jnp.transpose(summed[4], (0, 2, 1)),
    )


def solution(mesh):
    placed = (
        P(("dp", "row"), "col"),
        P("dp", None),
        P(("dp", "row"), "col"),
        P(None, "col"),
        P(None, "row", "col"),
        P(None, "row", "col"),
        P(None, "row", None),
        P(None, "row", "col"),
        P(None, "col", None),
        P(None, "col"),
        P(),
        P(),
        P(None, "col"),
        P(None, "col"),
        P(None, "col"),
        P(None, "col"),
        P(None, "col", "row"),
    )
    return jax.shard_map(
        local,
        mesh=mesh,
        in_specs=placed,
        out_specs=(
            P(("dp", "row"), "col"),
            P(("dp", "row"), "col"),
            P(None, "col"),
            P(None, ("dp", "row"), "col"),
            P(None, ("dp", "row"), "col"),
            P(None, ("dp", "row"), "col"),
            P(None, ("dp", "row"), "col"),
            P(None, "col", None),
            P(None, "col"),
            P(None, "col", None),
            P(None, "col"),
            P(None, "col"),
            P(None, "col"),
            P(None, "col"),
            P(None, "col"),
            P(None, "col", ("dp", "row")),
        ),
        check_vma=False,
    )
```

profile of v0, /device:TPU:0, one launch (start us, length us, event | category | flops | bytes accessed | tf_op | source)
XLA Modules:
  0.0 722.2 jit_solution(5391336732707727866)
XLA Ops:
  7.2 2.3 fusion.331
  13.2 13.5 %psum.119 = f32[256]{0:T(256)S(1)} all-reduce(f32[256]{0:T(256)S(1)} %fusion.178), channel_id=1, replica_groups=mesh['dp'=4,'row'=2,'col'=4] {'col'}, use_global_device_ids=true, to_apply=%region_1.0 | all-reduce | flops 256 | bytes 2048 | tf_op jit(solution)/shard_map/psum | solution.py:38
  27.4 14.8 %all_gather.84 = bf16[256,1024]{1,0:T(8,128)(2,1)S(1)} all-gather(bf16[256,256]{1,0:T(8,128)(2,1)S(1)} %fusion.180), channel_id=1, replica_groups=mesh['dp'=4,'row'=2,'col'=4] {'col'}, dimensions={1}, use_global_device_ids=true | all-gather | bytes 655360 | tf_op jit(solution)/shard_map/all_gather | solution.py:178
  42.9 12.6 %all-gather.1 = bf16[1,1024,256]{2,1,0:T(8,128)(2,1)S(1)} all-gather(bf16[1,512,256]{2,1,0:T(8,128)(2,1)S(1)} %get-tuple-element.584), channel_id=3, replica_groups=mesh['dp'=4,'row'=2,'col'=4] {'row'}, dimensions={1}, use_global_device_ids=true | all-gather | bytes 786432 | tf_op jit(solution)/shard_map/all_gather | solution.py:170
  59.3 4.4 all-gather.2
  72.6 3.5 collective-permute-start
  76.2 4.3 all-gather.3
  83.0 7.0 all-gather.4
  91.2 3.6 fusion.41
  95.0 2.7 multiply_reduce_fusion.15
  97.7 8.4 %psum.120 = f32[256]{0:T(256)S(1)} all-reduce(f32[256]{0:T(256)S(1)} %get-tuple-element.569), channel_id=1, replica_groups=mesh['dp'=4,'row'=2,'col'=4] {'col'}, use_global_device_ids=true, to_apply=%region_7.8 | all-reduce | flops 256 | bytes 2048 | tf_op jit(solution)/shard_map/psum | solution.py:38
  106.7 2.8 fusion.65
  111.6 7.0 all-gather.8
  118.6 4.4 all-gather.9
  123.0 19.0 %all_gather.100 = bf16[256,1024]{1,0:T(8,128)(2,1)} all-gather(bf16[256,256]{1,0:T(8,128)(2,1)S(1)} %copy-done.49), channel_id=1, replica_groups=mesh['dp'=4,'row'=2,'col'=4] {'col'}, dimensions={1}, use_global_device_ids=true | all-gather | bytes 655360 | tf_op jit(solution)/shard_map/all_gather | solution.py:292
  145.0 10.4 %psum.121 = f32[256]{0:T(256)S(1)} all-reduce(f32[256]{0:T(256)S(1)} %get-tuple-element.567), channel_id=1, replica_groups=mesh['dp'=4,'row'=2,'col'=4] {'col'}, use_global_device_ids=true, to_apply=%region_10.11 | all-reduce | flops 256 | bytes 2048 | tf_op jit(solution)/shard_map/psum | solution.py:38
  155.6 16.0 %all_gather.92 = bf16[256,1024]{1,0:T(8,128)(2,1)S(1)} all-gather(bf16[256,256]{1,0:T(8,128)(2,1)S(1)} %multiply_convert_fusion.4), channel_id=1, replica_groups=mesh['dp'=4,'row'=2,'col'=4] {'col'}, dimensions={1}, use_global_device_ids=true | all-gather | bytes 655360 | tf_op jit(solution)/shard_map/all_gather | solution.py:178
  178.8 4.6 all-gather.10
  185.6 2.4 divide_multiply_fusion
  190.9 7.2 all-gather.11
  200.3 4.6 fusion.32
  204.9 2.1 copy.148
  206.9 2.8 multiply_reduce_fusion.14
  209.7 10.2 %psum.122 = f32[256]{0:T(256)S(1)} all-reduce(f32[256]{0:T(256)S(1)} %get-tuple-element.561), channel_id=1, replica_groups=mesh['dp'=4,'row'=2,'col'=4] {'col'}, use_global_device_ids=true, to_apply=%region_16.17 | all-reduce | flops 256 | bytes 2048 | tf_op jit(solution)/shard_map/psum | solution.py:38
  219.9 3.4 multiply_reduce_fusion.6
  223.3 8.5 %psum.123 = f32[256]{0:T(256)S(1)} all-reduce(f32[256]{0:T(256)S(1)} %get-tuple-element.475), channel_id=1, replica_groups=mesh['dp'=4,'row'=2,'col'=4] {'col'}, use_global_device_ids=true, to_apply=%region_19.20 | all-reduce | flops 256 | bytes 2048 | tf_op jit(solution)/shard_map/psum | solution.py:38
  231.8 3.4 multiply_reduce_fusion.8
  235.2 2.1 copy.150
  240.2 7.2 all-gather.14
  248.7 2.4 multiply_reduce_fusion.5
  258.9 5.1 fusion.49
  268.1 4.3 fusion.26
  272.9 2.5 reduce-window.50
  277.5 2.0 copy.155
  279.7 2.7 fusion.56
  282.4 3.7 reduce-scatter.34.cloned.1.call-done
  287.1 2.6 fusion.117
  292.1 3.2 collective-permute-done.2
  304.5 18.3 %reduce-scatter.20.cloned.1.call-done = f32[256,256]{1,0:T(8,128)} async-done(((f32[256,1024]{1,0:T(8,128)}), f32[256,256]{1,0:T(8,128)}) %reduce-scatter.20.cloned.1.call-update) | async-done | bytes 262160 | tf_op jit(solution)/shard_map/reduce_scatter | solution.py:398
  324.6 9.5 %psum.124 = f32[256]{0:T(256)S(1)} all-reduce(f32[256]{0:T(256)S(1)} %get-tuple-element.479), channel_id=1, replica_groups=mesh['dp'=4,'row'=2,'col'=4] {'col'}, use_global_device_ids=true, to_apply=%region_37.39 | all-reduce | flops 256 | bytes 2048 | tf_op jit(solution)/shard_map/psum | solution.py:38
  335.7 14.9 %all_gather.103 = bf16[256,1024]{1,0:T(8,128)(2,1)S(1)} all-gather(bf16[256,256]{1,0:T(8,128)(2,1)S(1)} %fusion.315), channel_id=1, replica_groups=mesh['dp'=4,'row'=2,'col'=4] {'col'}, dimensions={1}, use_global_device_ids=true | all-gather | bytes 655360 | tf_op jit(solution)/shard_map/all_gather | solution.py:292
  350.6 3.3 multiply_reduce_fusion.7
  353.9 10.5 %psum.125 = f32[256]{0:T(256)S(1)} all-reduce(f32[256]{0:T(256)S(1)} %get-tuple-element.473), channel_id=1, replica_groups=mesh['dp'=4,'row'=2,'col'=4] {'col'}, use_global_device_ids=true, to_apply=%region_39.41 | all-reduce | flops 256 | bytes 2048 | tf_op jit(solution)/shard_map/psum | solution.py:38
  365.1 3.2 multiply_reduce_fusion.9
  372.7 7.2 all-gather.15
  389.0 5.2 fusion.51
  396.8 3.6 fusion.35
  401.0 2.5 reduce-window.56
  405.3 2.7 fusion.67
  408.0 5.6 reduce-scatter.36.cloned.1.call-done
  419.5 3.3 collective-permute-done.3
  425.8 2.8 fusion.54
  430.3 2.4 pad_maximum_fusion.2
  436.9 2.4 pad_maximum_fusion
  440.3 2.4 pad_maximum_fusion.1
  444.2 6.1 reduce-scatter.22.cloned.1.call-done
  451.5 9.6 %psum.126 = f32[256]{0:T(256)S(1)} all-reduce(f32[256]{0:T(256)S(1)} %get-tuple-element.481), channel_id=1, replica_groups=mesh['dp'=4,'row'=2,'col'=4] {'col'}, use_global_device_ids=true, to_apply=%region_57.59 | all-reduce | flops 256 | bytes 2048 | tf_op jit(solution)/shard_map/psum | solution.py:38
  461.0 25.9 %all-reduce.6 = (f32[2,256]{1,0:T(2,128)}, f32[2,512,4]{1,2,0:T(4,128)}, f32[2,512]{1,0:T(2,128)}, f32[2,64,4]{1,2,0:T(4,128)}, f32[2,64]{1,0:T(2,128)}, /*index...) all-reduce(f32[2,256]{1,0:T(2,128)S(1)} %pad_maximum_fusion.25, ...), channel_id=1, replica_groups=mesh['dp'=4,'row'=2,'col'=4] {'dp','row'}, use_global_device_ids=true, to_apply=%region_60.62 | all-reduce | flops 7344 | bytes 58752 | tf_op jit(solution)/shard_map/psum | solution.py:446
  487.1 2.0 fusion.182
  489.1 42.8 %reduce-scatter.32.cloned.1.call-done = f32[2,128,512]{2,1,0:T(8,128)} async-done(((f32[2,1024,512]{2,1,0:T(8,128)}), f32[2,128,512]{2,1,0:T(8,128)}) %reduce-scatter.32.cloned.1.call-update) | async-done | bytes 524304 | tf_op jit(solution)/shard_map/reduce_scatter | solution.py:444
  533.9 33.1 %reduce-scatter.30.cloned.1.call-done = f32[2,128,8]{1,2,0:T(8,128)} async-done(((f32[2,1024,8]{1,2,0:T(8,128)}), f32[2,128,8]{1,2,0:T(8,128)}) %reduce-scatter.30.cloned.1.call-update) | async-done | bytes 8208 | tf_op jit(solution)/shard_map/reduce_scatter | solution.py:443
  567.0 37.6 %reduce-scatter.28.cloned.1.call-done = f32[2,128,64]{1,2,0:T(8,128)} async-done(((f32[2,1024,64]{1,2,0:T(8,128)}), f32[2,128,64]{1,2,0:T(8,128)}) %reduce-scatter.28.cloned.1.call-update) | async-done | bytes 65552 | tf_op jit(solution)/shard_map/reduce_scatter | solution.py:442
  604.6 55.5 %reduce-scatter.24.cloned.1.call-done = f32[2,128,512]{2,1,0:T(8,128)} async-done(((f32[2,1024,512]{2,1,0:T(8,128)}), f32[2,128,512]{2,1,0:T(8,128)}) %reduce-scatter.24.cloned.1.call-update) | async-done | bytes 524304 | tf_op jit(solution)/shard_map/reduce_scatter | solution.py:440
  660.1 55.1 %reduce-scatter.26.cloned.1.call-done = f32[2,128,512]{2,1,0:T(8,128)} async-done(((f32[2,1024,512]{2,1,0:T(8,128)}), f32[2,128,512]{2,1,0:T(8,128)}) %reduce-scatter.26.cloned.1.call-update) | async-done | bytes 524304 | tf_op jit(solution)/shard_map/reduce_scatter | solution.py:441
  (633 shorter events, 115.8 us)
Async XLA Ops:
  7.2 63.7 %all-gather.23.cloned.1.call-start = ((), (), s32[]{:S(2)}) async-start(), calls=%async_computation.20 | async-start | bytes 1572864 | tf_op jit(solution)/shard_map/all_gather | solution.py:169
  9.6 85.4 %all-gather.25.cloned.1.call-start = ((), (), s32[]{:S(2)}) async-start(), calls=%async_computation.21 | async-start | bytes 1572864 | tf_op jit(solution)/shard_map/all_gather | solution.py:168
  10.7 31.5 %copy-start.57 = (bf16[2,512,256]{2,1,0:T(8,128)(2,1)S(1)}, bf16[2,512,256]{2,1,0:T(8,128)(2,1)}, u32[]{:S(2)}) copy-start(bf16[2,512,256]{2,1,0:T(8,128)(2,1)} %param.32) | copy-start | bytes 1572868
  10.7 95.5 %all-gather.27.cloned.1.call-start = ((), (), s32[]{:S(2)}) async-start(), calls=%async_computation.22 | async-start | bytes 1572864 | tf_op jit(solution)/shard_map/all_gather | solution.py:172
  12.2 43.3 %copy-start.142 = (f32[2,256,4]{1,2,0:T(4,128)S(1)}, f32[2,256,4]{1,2,0:T(4,128)}, u32[]{:S(2)}) copy-start(f32[2,256,4]{1,2,0:T(4,128)} %param.36) | copy-start | bytes 24580
  12.2 44.0 %copy-start.111 = (f32[2,512,4]{1,2,0:T(4,128)S(1)}, f32[2,512,4]{1,2,0:T(4,128)}, u32[]{:S(2)}) copy-start(f32[2,512,4]{1,2,0:T(4,128)} %param.34) | copy-start | bytes 49156
  12.2 45.4 %copy-start.172 = (f32[2,256]{1,0:T(2,128)S(1)}, f32[2,256]{1,0:T(2,128)}, u32[]{:S(2)}) copy-start(f32[2,256]{1,0:T(2,128)} %param.37) | copy-start | bytes 6148
  12.2 45.9 %copy-start.164 = (f32[2,512]{1,0:T(2,128)S(1)}, f32[2,512]{1,0:T(2,128)}, u32[]{:S(2)}) copy-start(f32[2,512]{1,0:T(2,128)} %param.35) | copy-start | bytes 12292
  12.2 46.5 %copy-start.162 = (f32[2,8]{1,0:T(2,128)S(1)}, f32[2,8]{1,0:T(2,128)}, u32[]{:S(2)}) copy-start(f32[2,8]{1,0:T(2,128)} %param.39) | copy-start | bytes 196
  12.2 47.0 %copy-start.112 = (bf16[2,512,8]{1,2,0:T(8,128)(2,1)S(1)}, bf16[2,512,8]{1,2,0:T(8,128)(2,1)}, u32[]{:S(2)}) copy-start(bf16[2,512,8]{1,2,0:T(8,128)(2,1)} %param.33) | copy-start | bytes 49156
  12.2 51.4 %copy-start.177 = (f32[2,8]{1,0:T(2,128)S(1)}, f32[2,8]{1,0:T(2,128)}, u32[]{:S(2)}) copy-start(f32[2,8]{1,0:T(2,128)} %param.38) | copy-start | bytes 196
  12.3 131.7 %reduce-scatter.16.cloned.1.call-start = ((), (), s32[]{:S(2)}) async-start(), calls=%async_computation.11 | async-start | bytes 1310720 | tf_op jit(solution)/shard_map/reduce_scatter | solution.py:230
  13.1 51.4 %copy-start.116 = (f32[1,256]{1,0:T(1,128)}, f32[1,256]{1,0:T(1,128)S(1)}, u32[]{:S(2)}) copy-start(f32[1,256]{1,0:T(1,128)S(1)} %get-tuple-element.623) | copy-start | bytes 3076
  13.1 142.3 %copy-start.86 = (f32[1,256]{1,0:T(1,128)}, f32[1,256]{1,0:T(1,128)S(1)}, u32[]{:S(2)}) copy-start(f32[1,256]{1,0:T(1,128)S(1)} %get-tuple-element.622) | copy-start | bytes 3076
  42.2 28.1 %copy-start.178 = (f32[2,8]{1,0:T(2,128)S(1)}, f32[2,8]{1,0:T(2,128)}, u32[]{:S(2)}) copy-start(f32[2,8]{1,0:T(2,128)} %param.40) | copy-start | bytes 196
  42.2 28.7 %copy-start.165 = (f32[2,512]{1,0:T(2,128)S(1)}, f32[2,512]{1,0:T(2,128)}, u32[]{:S(2)}) copy-start(f32[2,512]{1,0:T(2,128)} %param.41) | copy-start | bytes 12292
  64.9 26.3 %copy-start.143 = (f32[8,256]{1,0:T(8,128)}, f32[8,256]{1,0:T(8,128)S(1)}, u32[]{:S(2)}) copy-start(f32[8,256]{1,0:T(8,128)S(1)} %get-tuple-element.604) | copy-start | bytes 24580
  68.2 105.6 %copy-start.80 = (f32[256]{0:T(256)}, f32[256]{0:T(256)S(1)}, u32[]{:S(2)}) copy-start(f32[256]{0:T(256)S(1)} %get-tuple-element.613) | copy-start | bytes 3076
  68.2 223.1 %copy-start.64 = (f32[256]{0:T(256)}, f32[256]{0:T(256)S(1)}, u32[]{:S(2)}) copy-start(f32[256]{0:T(256)S(1)} %get-tuple-element.614) | copy-start | bytes 3076
  68.3 230.0 %copy-start.68 = (f32[256,8]{0,1:T(8,128)}, f32[256,8]{0,1:T(8,128)S(1)}, u32[]{:S(2)}) copy-start(f32[256,8]{0,1:T(8,128)S(1)} %get-tuple-element.571) | copy-start | bytes 24580
  70.9 35.3 %copy-start.69 = (f32[1,512]{1,0:T(1,128)}, f32[1,512]{1,0:T(1,128)S(1)}, u32[]{:S(2)}) copy-start(f32[1,512]{1,0:T(1,128)S(1)} %get-tuple-element.610) | copy-start | bytes 6148
  70.9 160.9 %copy-start.71 = (f32[1,512]{1,0:T(1,128)}, f32[1,512]{1,0:T(1,128)S(1)}, u32[]{:S(2)}) copy-start(f32[1,512]{1,0:T(1,128)S(1)} %get-tuple-element.609) | copy-start | bytes 6148
  72.6 7.9 %collective-permute-start = (f32[3,768]{1,0:T(4,128)S(1)}, f32[3,768]{1,0:T(4,128)S(1)}, u32[]{:S(2)}, u32[]{:S(2)}) collective-permute-start(f32[3,768]{1,0:T(4,128)S(1)} %fusion.242), channel_id=1, source_target_pairs={{0,4},{1,5},{2,6},{3,7},{8,12},{9,13},{10,14},{11,15},{16,20},{17,... | collective-permute-start | bytes 27656 | tf_op jit(solution)/shard_map/ppermute | solution.py:18
  80.6 219.4 %copy-start = (f32[259,768]{1,0:T(8,128)}, f32[259,768]{1,0:T(8,128)S(1)}, u32[]{:S(2)}) copy-start(f32[259,768]{1,0:T(8,128)S(1)} %maximum_maximum_fusion) | copy-start | bytes 2386948
  109.5 32.5 %copy-start.113 = (f32[256,4]{0,1:T(4,128)S(1)}, f32[256,4]{0,1:T(4,128)}, u32[]{:S(2)}) copy-start(f32[256,4]{0,1:T(4,128)} %get-tuple-element.595) | copy-start | bytes 12292
  109.5 33.1 %copy-start.129 = (f32[1,256,4]{1,2,0:T(4,128)S(1)}, f32[1,256,4]{1,2,0:T(4,128)}, u32[]{:S(2)}) copy-start(f32[1,256,4]{1,2,0:T(4,128)} %get-tuple-element.596) | copy-start | bytes 12292
  109.5 33.8 %copy-start.153 = (f32[1,512]{1,0:T(1,128)S(1)}, f32[1,512]{1,0:T(1,128)}, u32[]{:S(2)}) copy-start(f32[1,512]{1,0:T(1,128)} %get-tuple-element.611) | copy-start | bytes 6148
  109.5 33.8 %copy-start.166 = (f32[1,256]{1,0:T(1,128)S(1)}, f32[1,256]{1,0:T(1,128)}, u32[]{:S(2)}) copy-start(f32[1,256]{1,0:T(1,128)} %get-tuple-element.620) | copy-start | bytes 3076
  109.5 34.4 %copy-start.29 = (bf16[256,256]{1,0:T(8,128)(2,1)S(1)}, bf16[256,256]{1,0:T(8,128)(2,1)}, u32[]{:S(2)}) copy-start(bf16[256,256]{1,0:T(8,128)(2,1)} %param.26) | copy-start | bytes 393220
  109.6 64.7 %all-gather.29.cloned.1.call-start = ((), (), s32[]{:S(2)}) async-start(), calls=%async_computation.23 | async-start | bytes 1572864 | tf_op jit(solution)/shard_map/all_gather | solution.py:169
  110.2 96.8 %all-gather.31.cloned.1.call-start = ((), (), s32[]{:S(2)}) async-start(), calls=%async_computation.24 | async-start | bytes 1572864 | tf_op jit(solution)/shard_map/all_gather | solution.py:168
  110.2 61.3 %copy-start.168 = (f32[8]{0:T(128)S(1)}, f32[8]{0:T(128)}, u32[]{:S(2)}) copy-start(f32[8]{0:T(128)} %get-tuple-element.630) | copy-start | bytes 100
  110.7 109.1 %all-gather.33.cloned.1.call-start = ((), (), s32[]{:S(2)}) async-start(), calls=%async_computation.25 | async-start | bytes 1572864 | tf_op jit(solution)/shard_map/all_gather | solution.py:172
  110.8 61.0 %copy-start.159 = (f32[8]{0:T(128)S(1)}, f32[8]{0:T(128)}, u32[]{:S(2)}) copy-start(f32[8]{0:T(128)} %get-tuple-element.628) | copy-start | bytes 100
  111.5 174.6 %reduce-scatter.34.cloned.1.call-start = ((), (), s32[]{:S(2)}) async-start(), calls=%async_computation.26 | async-start | bytes 327680
  118.6 55.6 %copy-start.33 = (bf16[1,1024,256]{2,1,0:T(8,128)(2,1)}, bf16[1,1024,256]{2,1,0:T(8,128)(2,1)S(1)}, u32[]{:S(2)}) copy-start(bf16[1,1024,256]{2,1,0:T(8,128)(2,1)S(1)} %all-gather.8) | copy-start | bytes 1572868
  155.4 20.6 %copy-start.126 = (f32[256]{0:T(256)}, f32[256]{0:T(256)S(1)}, u32[]{:S(2)}) copy-start(f32[256]{0:T(256)S(1)} %psum.121) | copy-start | bytes 3076
  155.4 20.6 %copy-start.83 = (f32[256]{0:T(256)}, f32[256]{0:T(256)S(1)}, u32[]{:S(2)}) copy-start(f32[256]{0:T(256)S(1)} %add_rsqrt_fusion.1) | copy-start | bytes 3076
  176.1 8.4 %collective-permute-start.1 = (f32[3,768]{1,0:T(4,128)S(1)}, f32[3,768]{1,0:T(4,128)}, u32[]{:S(2)}, u32[]{:S(2)}) collective-permute-start(f32[3,768]{1,0:T(4,128)S(1)} %fusion.241), channel_id=1, source_target_pairs={{0,4},{1,5},{2,6},{3,7},{8,12},{9,13},{10,14},{11,15},{16,20},{17,... | collective-permute-start | bytes 27656 | tf_op jit(solution)/shard_map/ppermute | solution.py:18
  268.0 54.9 %reduce-scatter.20.cloned.1.call-start = ((), (), s32[]{:S(2)}) async-start(), calls=%async_computation.13 | async-start | bytes 1310720 | tf_op jit(solution)/shard_map/reduce_scatter | solution.py:398
  289.8 5.6 collective-permute-start.2
  298.2 115.4 %reduce-scatter.36.cloned.1.call-start = ((), (), s32[]{:S(2)}) async-start(), calls=%async_computation.27 | async-start | bytes 327680
  299.3 23.5 %copy-start.14 = (f32[256,256]{1,0:T(8,128)S(1)}, f32[256,256]{1,0:T(8,128)}, u32[]{:S(2)}) copy-start(f32[256,256]{1,0:T(8,128)} %copy-done.13) | copy-start | bytes 786436
  299.3 23.5 %copy-start.84 = (f32[256]{0:T(256)S(1)}, f32[256]{0:T(256)}, u32[]{:S(2)}) copy-start(f32[256]{0:T(256)} %copy-done.83) | copy-start | bytes 3076
  299.3 23.5 %copy-start.87 = (f32[1,256]{1,0:T(1,128)S(1)}, f32[1,256]{1,0:T(1,128)}, u32[]{:S(2)}) copy-start(f32[1,256]{1,0:T(1,128)} %copy-done.86) | copy-start | bytes 3076
  300.1 34.0 %copy-start.127 = (f32[256]{0:T(256)S(1)}, f32[256]{0:T(256)}, u32[]{:S(2)}) copy-start(f32[256]{0:T(256)} %copy-done.126) | copy-start | bytes 3076
  300.1 34.6 %copy-start.50 = (bf16[256,256]{1,0:T(8,128)(2,1)S(1)}, bf16[256,256]{1,0:T(8,128)(2,1)}, u32[]{:S(2)}) copy-start(bf16[256,256]{1,0:T(8,128)(2,1)} %param.28) | copy-start | bytes 393220
  300.1 50.5 %copy-start.11 = (f32[256,512]{1,0:T(8,128)S(1)}, f32[256,512]{1,0:T(8,128)}, u32[]{:S(2)}) copy-start(f32[256,512]{1,0:T(8,128)} %copy-done.10) | copy-start | bytes 1572868
  324.6 40.5 %copy-start.3 = (f32[256,768]{1,0:T(8,128)S(1)}, f32[256,768]{1,0:T(8,128)}, u32[]{:S(2)}) copy-start(f32[256,768]{1,0:T(8,128)} %copy-done.2) | copy-start | bytes 2359300
  396.4 54.0 %reduce-scatter.22.cloned.1.call-start = ((), (), s32[]{:S(2)}) async-start(), calls=%async_computation.14 | async-start | bytes 1310720 | tf_op jit(solution)/shard_map/reduce_scatter | solution.py:398
  417.3 5.6 collective-permute-start.3
  425.7 61.2 %reduce-scatter.18.cloned.1.call-start = ((), (), s32[]{:S(2)}) async-start(), calls=%async_computation.12 | async-start | bytes 1310720 | tf_op jit(solution)/shard_map/reduce_scatter | solution.py:230
  428.7 103.2 %reduce-scatter.32.cloned.1.call-start = ((), (), s32[]{:S(2)}) async-start(), calls=%async_computation.19 | async-start | bytes 4718592 | tf_op jit(solution)/shard_map/reduce_scatter | solution.py:444
  432.7 134.3 %reduce-scatter.30.cloned.1.call-start = ((), (), s32[]{:S(2)}) async-start(), calls=%async_computation.18 | async-start | bytes 73728 | tf_op jit(solution)/shard_map/reduce_scatter | solution.py:443
  434.7 169.9 %reduce-scatter.28.cloned.1.call-start = ((), (), s32[]{:S(2)}) async-start(), calls=%async_computation.17 | async-start | bytes 589824 | tf_op jit(solution)/shard_map/reduce_scatter | solution.py:442
  435.9 224.2 %reduce-scatter.24.cloned.1.call-start = ((), (), s32[]{:S(2)}) async-start(), calls=%async_computation.15 | async-start | bytes 4718592 | tf_op jit(solution)/shard_map/reduce_scatter | solution.py:440
  439.3 275.9 %reduce-scatter.26.cloned.1.call-start = ((), (), s32[]{:S(2)}) async-start(), calls=%async_computation.16 | async-start | bytes 4718592 | tf_op jit(solution)/shard_map/reduce_scatter | solution.py:441
  442.9 18.2 %copy-start.161 = (f32[256]{0:T(256)S(1)}, f32[256]{0:T(256)}, u32[]{:S(2)}) copy-start(f32[256]{0:T(256)} %get-tuple-element.478) | copy-start | bytes 3076
  442.9 44.1 %copy-start.124 = (f32[256]{0:T(256)S(1)}, f32[256]{0:T(256)}, u32[]{:S(2)}) copy-start(f32[256]{0:T(256)} %copy-done.123) | copy-start | bytes 3076
  442.9 44.1 %copy-start.15 = (f32[256,256]{1,0:T(8,128)S(1)}, f32[256,256]{1,0:T(8,128)}, u32[]{:S(2)}) copy-start(f32[256,256]{1,0:T(8,128)} %copy-done.13) | copy-start | bytes 786436
  442.9 44.1 %copy-start.41 = (f32[256,256]{1,0:T(8,128)S(1)}, f32[256,256]{1,0:T(8,128)}, u32[]{:S(2)}) copy-start(f32[256,256]{1,0:T(8,128)} %reduce-scatter.20.cloned.1.call-done) | copy-start | bytes 786436
  442.9 44.1 %copy-start.85 = (f32[256]{0:T(256)S(1)}, f32[256]{0:T(256)}, u32[]{:S(2)}) copy-start(f32[256]{0:T(256)} %copy-done.83) | copy-start | bytes 3076
  442.9 44.1 %copy-start.88 = (f32[1,256]{1,0:T(1,128)S(1)}, f32[1,256]{1,0:T(1,128)}, u32[]{:S(2)}) copy-start(f32[1,256]{1,0:T(1,128)} %copy-done.86) | copy-start | bytes 3076
  442.9 44.1 %copy-start.131 = (f32[256]{0:T(256)S(1)}, f32[256]{0:T(256)}, u32[]{:S(2)}) copy-start(f32[256]{0:T(256)} %copy-done.130) | copy-start | bytes 3076
  (146 other events, 994.4 us)
Sparse Core Ops, SparseCore 0:
  10.1 23.9 all-gather.22
  35.7 24.1 all-gather.24
  61.5 23.8 all-gather.26
  109.7 32.1 reduce-scatter.15
  144.0 20.0 all-gather.28
  166.1 21.3 all-gather.30
  189.1 23.2 all-gather.32
  268.1 17.9 reduce-scatter.33
  298.3 24.4 reduce-scatter.19
  396.5 17.0 reduce-scatter.35
  425.9 24.4 reduce-scatter.21
  452.6 25.7 reduce-scatter.17
  481.8 50.0 reduce-scatter.31
  535.6 31.3 reduce-scatter.29
  570.5 34.0 reduce-scatter.27
  608.8 51.3 reduce-scatter.23
  663.9 51.2 reduce-scatter.25
where the time goes:
time: 732 us; the launch traced here: 722 us
  waiting for transfers between devices  267 us (36%)
  blocking collectives  237 us (32%)
  matrix products  81.4 us (11%)
  other arithmetic  61.8 us (8%)
  local copies, waits for them, and re-layouts  47.9 us (7%)
  between operations  18.3 us (2%)
  starting transfers between devices  9.14 us (1%)
    psum x8, blocking collectives, row_total(): return lax.psum(values, 'col')  80.5 us
    reduce_scatter x1, waiting for transfers between devices, local(): lax.psum_scatter(stacked(grads_gate), ('dp', 'row'), scatter_dimension=1,...  55.5 us
    reduce_scatter x1, waiting for transfers between devices, local(): lax.psum_scatter(stacked(grads_inner), ('dp', 'row'), scatter_dimension=1...  55.1 us
    reduce_scatter x1, waiting for transfers between devices, local(): lax.psum_scatter(stacked(grads_out), ('dp', 'row'), scatter_dimension=1,...  42.8 us
    reduce_scatter x1, waiting for transfers between devices, local(): lax.psum_scatter(stacked(grads_pair), ('dp', 'row'), scatter_dimension=1,...  37.6 us
    all_gather x6, blocking collectives, carried_in(): gathered = jax.tree.map(lambda a: lax.all_gather(a, axis), part)  37.5 us
    all_gather x2, blocking collectives, local(): cot_all = lax.all_gather(cot_low, 'col', axis=1, tiled=True)  33.9 us
    reduce_scatter x1, waiting for transfers between devices, local(): lax.psum_scatter(stacked(grads_step), ('dp', 'row'), scatter_dimension=1,...  33.1 us
  transfers between devices with their start and end apart: 21, of which 11 were waited for; matrix products, arithmetic and copies ran while one was open for 14% of the time, Pallas kernels for 0%

commit v1 on v0

--- a/solution.py
+++ b/solution.py
@@ -1,6 +1,10 @@
+import functools
+
 import jax
 import jax.numpy as jnp
 from jax import lax
+from jax.experimental import pallas as pl
+from jax.experimental.pallas import tpu as pltpu
 from jax.sharding import PartitionSpec as P
 
 KERNEL = 4
@@ -21,6 +25,9 @@
 def carried_in(part, axis, combine, identity, reverse):
     count = lax.axis_size(axis)
     place = lax.axis_index(axis)
+    if count == 2:
+        moved = lax.ppermute(part[1], axis, [(1, 0)] if reverse else [(0, 1)])
+        return (None, moved)
     ahead = count - 1 - place if reverse else place
     gathered = jax.tree.map(lambda a: lax.all_gather(a, axis), part)
     state = jax.tree.map(lambda a, e: jnp.zeros_like(a) + jnp.asarray(e, a.dtype), part, identity)
@@ -34,8 +41,312 @@
     return lax.fori_loop(0, ahead, one, state)
 
 
+MESH = pl.DeviceIdType.MESH
+VMEM_SPEC = pl.BlockSpec(memory_space=pltpu.VMEM)
+ANY_SPEC = pl.BlockSpec(memory_space=pl.ANY)
+
+
+def greet(peers):
+    barrier = pltpu.get_barrier_semaphore()
+    for peer in peers:
+        pl.semaphore_signal(barrier, inc=1, device_id=peer, device_id_type=MESH)
+    pl.semaphore_wait(barrier, len(peers))
+
+
+def col_peers(n):
+    me = lax.axis_index("col")
+    return [{"col": lax.rem(me + k, n)} for k in range(1, n)]
+
+
+def start_to(peers, src_of, dst, send, recv):
+    copies = []
+    for k, peer in enumerate(peers):
+        copy = pltpu.make_async_remote_copy(
+            src_ref=src_of(peer),
+            dst_ref=dst,
+            send_sem=send.at[k],
+            recv_sem=recv.at[k],
+            device_id=peer,
+            device_id_type=MESH,
+        )
+        copy.start()
+        copies.append(copy)
+    return copies
+
+
+def row_sum_kernel(n, value_ref, total_ref, slots, send, recv):
+    me = lax.axis_index("col")
+    peers = col_peers(n)
+    slots[me] = value_ref[...]
+    greet(peers)
+    copies = start_to(peers, lambda peer: value_ref, slots.at[me], send, recv)
+    for copy in copies:
+        copy.wait()
+    total = slots[0]
+    for k in range(1, n):
+        total = total + slots[k]
+    total_ref[...] = total
+
+
 def row_total(values):
-    return lax.psum(values, "col")
+    n = lax.axis_size("col")
+    rows = values.shape[0]
+    out = pl.pallas_call(
+        functools.partial(row_sum_kernel, n),
+        out_shape=jax.ShapeDtypeStruct((1, rows), jnp.float32),
+        in_specs=[VMEM_SPEC],
+        out_specs=VMEM_SPEC,
+        scratch_shapes=[
+            pltpu.VMEM((n, 1, rows), jnp.float32),
+            pltpu.SemaphoreType.DMA((n - 1,)),
+            pltpu.SemaphoreType.DMA((n - 1,)),
+        ],
+        compiler_params=pltpu.CompilerParams(collective_id=0, has_side_effects=True),
+        name="row_total",
+    )(values.reshape(1, rows))
+    return out[0]
+
+
+def scatter_sum(n, part_ref, outgoing, arrived, send, recv):
+    me = lax.axis_index("col")
+    peers = col_peers(n)
+    width = outgoing.shape[2]
+    for k in range(n):
+        outgoing[k] = part_ref[:, k * width : (k + 1) * width].astype(outgoing.dtype)
+    greet(peers)
+    copies = start_to(peers, lambda peer: outgoing.at[peer["col"]], arrived.at[me], send, recv)
+    total = part_ref[:, pl.ds(pl.multiple_of(me * width, width), width)]
+    for copy in copies:
+        copy.wait()
+    for peer in peers:
+        total = total + arrived[peer["col"]].astype(jnp.float32)
+    return total
+
+
+def rows_over_col(n, product, row_own, row_slots, send, recv):
+    me = lax.axis_index("col")
+    peers = col_peers(n)
+    ones = jnp.ones((8, product.shape[1]), jnp.float32)
+    sums = lax.dot_general(
+        ones, product, (((1,), (1,)), ((), ())), precision=HIGHEST,
+        preferred_element_type=jnp.float32,
+    )
+    row_own[...] = sums
+    row_slots[me] = sums
+    copies = start_to(peers, lambda peer: row_own, row_slots.at[me], send, recv)
+    for copy in copies:
+        copy.wait()
+    total = row_slots[0]
+    for k in range(1, n):
+        total = total + row_slots[k]
+    return jnp.transpose(total)[:, :1]
+
+
+def gather_cols(n, own, all_ref, send, recv):
+    me = lax.axis_index("col")
+    peers = col_peers(n)
+    width = own.shape[1]
+    place = all_ref.at[:, pl.ds(pl.multiple_of(me * width, width), width)]
+    place[...] = own[...]
+    copies = start_to(peers, lambda peer: own, place, send, recv)
+    for copy in copies:
+        copy.wait()
+
+
+def forward_turn_kernel(
+    n, part_ref, resid_ref, gain_ref, resid_out, scale_out, normed_out,
+    outgoing, arrived, row_own, row_slots, own, *sems,
+):
+    resid = resid_ref[...] + scatter_sum(n, part_ref, outgoing, arrived, sems[0], sems[1])
+    resid_out[...] = resid
+    square = rows_over_col(n, resid * resid, row_own, row_slots, sems[2], sems[3])
+    scale = lax.rsqrt(square / (n * resid.shape[1]) + EPSILON)
+    scale_out[...] = scale
+    own[...] = (resid * scale * gain_ref[...]).astype(jnp.bfloat16)
+    gather_cols(n, own, normed_out, sems[4], sems[5])
+
+
+def backward_turn_kernel(
+    n, spread, part_ref, grad_ref, resid_ref, scale_ref, gain_ref, grad_out, gain_out, *rest
+):
+    if spread:
+        cot_out, rest = rest[0], rest[1:]
+    outgoing, arrived, row_own, row_slots, own = rest[:5]
+    sems = rest[5:]
+    d_normed = scatter_sum(n, part_ref, outgoing, arrived, sems[0], sems[1])
+    resid = resid_ref[...]
+    scale = scale_ref[...]
+    scaled_in = d_normed * gain_ref[...]
+    gain_out[...] = jnp.sum(d_normed * resid * scale, axis=0, keepdims=True)
+    total = rows_over_col(n, scaled_in * resid, row_own, row_slots, sems[2], sems[3])
+    grad = (
+        grad_ref[...]
+        + scale * scaled_in
+        - resid * (scale * scale * scale * total / (n * resid.shape[1]))
+    )
+    grad_out[...] = grad
+    if spread:
+        own[...] = grad.astype(jnp.bfloat16)
+        gather_cols(n, own, cot_out, sems[4], sems[5])
+
+
+def turn_scratch(n, rows, width):
+    return [
+        pltpu.VMEM((n, rows, width), jnp.bfloat16),
+        pltpu.VMEM((n, rows, width), jnp.bfloat16),
+        pltpu.VMEM((8, rows), jnp.float32),
+        pltpu.VMEM((n, 8, rows), jnp.float32),
+        pltpu.VMEM((rows, width), jnp.bfloat16),
+    ] + [pltpu.SemaphoreType.DMA((n - 1,)) for _ in range(6)]
+
+
+def forward_turn(part, resid, gain):
+    n = lax.axis_size("col")
+    rows, width = resid.shape
+    return pl.pallas_call(
+        functools.partial(forward_turn_kernel, n),
+        out_shape=[
+            jax.ShapeDtypeStruct((rows, width), jnp.float32),
+            jax.ShapeDtypeStruct((rows, 1), jnp.float32),
+            jax.ShapeDtypeStruct((rows, n * width), jnp.bfloat16),
+        ],
+        in_specs=[VMEM_SPEC] * 3,
+        out_specs=[VMEM_SPEC] * 3,
+        scratch_shapes=turn_scratch(n, rows, width),
+        compiler_params=pltpu.CompilerParams(collective_id=1, has_side_effects=True),
+        name="forward_turn",
+    )(part, resid, gain[None, :])
+
+
+def backward_turn(part, grad, resid, scale, gain, spread):
+    n = lax.axis_size("col")
+    rows, width = resid.shape
+    outs = [
+        jax.ShapeDtypeStruct((rows, width), jnp.float32),
+        jax.ShapeDtypeStruct((1, width), jnp.float32),
+    ]
+    if spread:
+        outs.append(jax.ShapeDtypeStruct((rows, n * width), jnp.bfloat16))
+    return pl.pallas_call(
+        functools.partial(backward_turn_kernel, n, spread),
+        out_shape=outs,
+        in_specs=[VMEM_SPEC] * 5,
+        out_specs=[VMEM_SPEC] * len(outs),
+        scratch_shapes=turn_scratch(n, rows, width),
+        compiler_params=pltpu.CompilerParams(
+            collective_id=2 if spread else 3, has_side_effects=True
+        ),
+        name="backward_turn" if spread else "backward_end",
+    )(part, grad, resid, scale[:, None], gain[None, :])
+
+
+def entry_kernel(n, tok_ref, gain_ref, tok_all, gain_all, *sems):
+    me = lax.axis_index("col")
+    peers = col_peers(n)
+    width = tok_ref.shape[1]
+    place = tok_all.at[:, pl.ds(pl.multiple_of(me * width, width), width)]
+    place[...] = tok_ref[...]
+    gain_all[me] = gain_ref[...]
+    greet(peers)
+    copies = start_to(peers, lambda peer: tok_ref, place, sems[0], sems[1])
+    copies += start_to(peers, lambda peer: gain_ref, gain_all.at[me], sems[2], sems[3])
+    for copy in copies:
+        copy.wait()
+
+
+def entry_gather(tokens, gain):
+    n = lax.axis_size("col")
+    rows, width = tokens.shape
+    return pl.pallas_call(
+        functools.partial(entry_kernel, n),
+        out_shape=[
+            jax.ShapeDtypeStruct((rows, n * width), tokens.dtype),
+            jax.ShapeDtypeStruct((n, 1, width), gain.dtype),
+        ],
+        in_specs=[VMEM_SPEC] * 2,
+        out_specs=[VMEM_SPEC] * 2,
+        scratch_shapes=[pltpu.SemaphoreType.DMA((n - 1,)) for _ in range(4)],
+        compiler_params=pltpu.CompilerParams(collective_id=4, has_side_effects=True),
+        name="entry_gather",
+    )(tokens, gain[None, :])
+
+
+def small_kernel(dp, row, value_ref, total_ref, slots, send, recv):
+    at_dp, at_row = lax.axis_index("dp"), lax.axis_index("row")
+    me = at_dp * row + at_row
+    peers = []
+    for k in range(1, dp * row):
+        peers.append(
+            {"dp": lax.rem(at_dp + k // row, dp), "row": lax.rem(at_row + k % row, row)}
+        )
+    slots[me] = value_ref[...]
+    greet(peers)
+    copies = start_to(peers, lambda peer: value_ref, slots.at[me], send, recv)
+    for copy in copies:
+        copy.wait()
+    total = slots[0]
+    for k in range(1, dp * row):
+        total = total + slots[k]
+    total_ref[...] = total
+
+
+def small_total(value):
+    dp, row = lax.axis_size("dp"), lax.axis_size("row")
+    count = dp * row
+    if count > 8:
+        return lax.psum(value, ("dp", "row"))
+    return pl.pallas_call(
+        functools.partial(small_kernel, dp, row),
+        out_shape=jax.ShapeDtypeStruct(value.shape, jnp.float32),
+        in_specs=[VMEM_SPEC],
+        out_specs=VMEM_SPEC,
+        scratch_shapes=[
+            pltpu.VMEM((count,) + value.shape, jnp.float32),
+            pltpu.SemaphoreType.DMA((count - 1,)),
+            pltpu.SemaphoreType.DMA((count - 1,)),
+        ],
+        compiler_params=pltpu.CompilerParams(collective_id=5, has_side_effects=True),
+        name="small_total",
+    )(value)
+
+
+def whole_over_row(block, axis):
+    if lax.axis_size("row") != 2:
+        return lax.all_gather(block, "row", axis=axis, tiled=True)
+    other = lax.ppermute(block, "row", [(0, 1), (1, 0)])
+    size = block.shape[axis]
+    trio = jnp.concatenate([block, other, block], axis=axis)
+    return lax.dynamic_slice_in_dim(trio, lax.axis_index("row") * size, 2 * size, axis)
+
+
+def whole_over_col(block):
+    n = lax.axis_size("col")
+    size = block.shape[1]
+    blocks = [block]
+    for k in range(1, n):
+        blocks.append(lax.ppermute(block, "col", [(i, (i - k) % n) for i in range(n)]))
+    twice = jnp.concatenate(blocks + blocks[:-1], axis=1)
+    start = lax.rem(n - lax.axis_index("col"), n) * size
+    return lax.dynamic_slice_in_dim(twice, start, n * size, 1)
+
+
+def packed_small(parts):
+    flat = jnp.concatenate([part.reshape(-1) for part in parts])
+    total = flat.shape[0]
+    lines = -(-total // 1024) * 8
+    return jnp.pad(flat, (0, lines * 128 - total)).reshape(lines, 128)
+
+
+def unpacked_small(packed, shapes):
+    flat = packed.reshape(-1)
+    out, at = [], 0
+    for shape in shapes:
+        size = 1
+        for extent in shape:
+            size *= extent
+        out.append(flat[at : at + size].reshape(shape))
+        at += size
+    return out
 
 
 def link_up(earlier, later):
@@ -162,20 +473,24 @@
     dims_t = (((1,), (1,)), ((), ()))
     dims_w = (((0,), (0,)), ((), ()))
     resid = tokens.astype(jnp.float32)
+    tokens_all, gain_all = entry_gather(tokens, norm_gain[0])
+    first_all = tokens_all.astype(jnp.float32)
+    row_scale = lax.rsqrt(jnp.sum(first_all * first_all, axis=1) / full_width + EPSILON)
+    normed_all = (first_all * row_scale[:, None] * gain_all.reshape(1, -1)).astype(jnp.bfloat16)
+    whole_weights = [
+        (
+            whole_over_row(gate_weight[layer_at], 0),
+            whole_over_row(inner_weight[layer_at], 0),
+            whole_over_row(state_weight[layer_at], 0),
+            whole_over_row(step_weight[layer_at], 0),
+            whole_over_row(output_weight[layer_at], 1),
+        )
+        for layer_at in range(LAYERS)
+    ]
+    cot_all = whole_over_col(cotangent)
     saved = []
     for layer_at in range(LAYERS):
-        gathered = (
-            lax.all_gather(gate_weight[layer_at], "row", axis=0, tiled=True),
-            lax.all_gather(inner_weight[layer_at], "row", axis=0, tiled=True),
-            lax.all_gather(state_weight[layer_at], "row", axis=0, tiled=True),
-            lax.all_gather(step_weight[layer_at], "row", axis=0, tiled=True),
-            lax.all_gather(output_weight[layer_at], "row", axis=1, tiled=True),
-        )
-        gate_full, inner_whole, state_full, step_full, output_full = gathered
-        square = row_total(jnp.sum(resid * resid, axis=1))
-        row_scale = lax.rsqrt(square / full_width + EPSILON)
-        normed = (resid * row_scale[:, None] * norm_gain[layer_at][None, :]).astype(jnp.bfloat16)
-        normed_all = lax.all_gather(normed, "col", axis=1, tiled=True)
+        gate_full, inner_whole, state_full, step_full, output_full = whole_weights[layer_at]
         gate_val = jnp.dot(normed_all, gate_full, preferred_element_type=jnp.float32)
         inner_val = jnp.dot(normed_all, inner_whole, preferred_element_type=jnp.float32)
         pair_val = jnp.dot(normed_all, state_full, preferred_element_type=jnp.float32)
@@ -227,7 +542,6 @@
             jnp.bfloat16
         )
         partial_out = jnp.dot(normed_y, output_full, preferred_element_type=jnp.float32)
-        branch = lax.psum_scatter(partial_out, "col", scatter_dimension=1, tiled=True)
         stored = None
         saved.append(
             (
@@ -253,11 +567,17 @@
                 stored,
             )
         )
-        resid = resid + branch
+        if layer_at + 1 < LAYERS:
+            resid, new_scale, normed_all = forward_turn(
+                partial_out, resid, norm_gain[layer_at + 1]
+            )
+            row_scale = new_scale[:, 0]
+        else:
+            resid = resid + lax.psum_scatter(partial_out, "col", scatter_dimension=1, tiled=True)
     layer_output = resid.astype(jnp.bfloat16)
     resid_grad = cotangent.astype(jnp.float32)
-    grads_gate, grads_inner, grads_pair, grads_step, grads_out = ([], [], [], [], [])
-    small_terms = []
+    big_grads = [None] * LAYERS
+    small_terms = [None] * LAYERS
     for layer_at in reversed(range(LAYERS)):
         (
             resid,
@@ -281,21 +601,11 @@
             normed_y,
             stored,
         ) = saved[layer_at]
-        gate_full, inner_whole, state_full, step_full, output_full = (
-            lax.all_gather(gate_weight[layer_at], "row", axis=0, tiled=True),
-            lax.all_gather(inner_weight[layer_at], "row", axis=0, tiled=True),
-            lax.all_gather(state_weight[layer_at], "row", axis=0, tiled=True),
-            lax.all_gather(step_weight[layer_at], "row", axis=0, tiled=True),
-            lax.all_gather(output_weight[layer_at], "row", axis=1, tiled=True),
-        )
-        cot_low = resid_grad.astype(jnp.bfloat16)
-        cot_all = lax.all_gather(cot_low, "col", axis=1, tiled=True)
+        gate_full, inner_whole, state_full, step_full, output_full = whole_weights[layer_at]
         d_normed_y = lax.dot_general(
             cot_all, output_full, dims_t, preferred_element_type=jnp.float32
         )
-        grads_out.append(
-            lax.dot_general(cot_all, normed_y, dims_w, preferred_element_type=jnp.float32)
-        )
+        grad_out = lax.dot_general(cot_all, normed_y, dims_w, preferred_element_type=jnp.float32)
         scaled_y = d_normed_y * gated_gain[layer_at][None, :]
         total_y = row_total(jnp.sum(scaled_y * gated, axis=1))
         d_gated = (
@@ -376,7 +686,7 @@
             kernel_terms.append(
                 jnp.sum(d_pre * own_padded[offset : offset + tok_rows] * same_fwd[:, None], axis=0)
             )
-        kernel_grad = jnp.stack(kernel_terms, axis=1)
+        kernel_grad = jnp.stack(kernel_terms, axis=0)
         bias_grad = jnp.sum(d_pre, axis=0)
         d_gate16 = d_gate.astype(jnp.bfloat16)
         d_inner16 = d_values[:, :inner_cols].astype(jnp.bfloat16)
@@ -395,85 +705,65 @@
         partial_in = partial_in + lax.dot_general(
             d_step16, step_full, dims_t, preferred_element_type=jnp.float32
         )
-        d_normed = lax.psum_scatter(partial_in, "col", scatter_dimension=1, tiled=True)
-        grads_gate.append(
-            lax.dot_general(normed_all, d_gate16, dims_w, preferred_element_type=jnp.float32)
-        )
-        grads_inner.append(
-            lax.dot_general(normed_all, d_inner16, dims_w, preferred_element_type=jnp.float32)
-        )
-        grads_pair.append(
-            lax.dot_general(normed_all, d_pair16, dims_w, preferred_element_type=jnp.float32)
-        )
-        grads_step.append(
-            lax.dot_general(normed_all, d_step16, dims_w, preferred_element_type=jnp.float32)
-        )
-        scaled_in = d_normed * norm_gain[layer_at][None, :]
-        total_in = row_total(jnp.sum(scaled_in * resid, axis=1))
-        gain_in = jnp.sum(d_normed * resid * row_scale[:, None], axis=0)
-        resid_grad = (
-            resid_grad
-            + row_scale[:, None] * scaled_in
-            - resid * (row_scale**3 * total_in / full_width)[:, None]
-        )
-        small_terms.append(
-            (
-                gain_in,
-                gain_y,
-                kernel_grad[:inner_cols],
-                bias_grad[:inner_cols],
-                kernel_grad[inner_cols:],
-                bias_grad[inner_cols:],
-                g_step_bias,
-                g_decay,
-                g_skip,
-            )
-        )
-
-    def stacked(items):
-        return jnp.stack(items[::-1], axis=0)
-
-    def column(slot):
-        return jnp.stack([terms[slot] for terms in small_terms[::-1]], axis=0)
-
-    summed = (
-        lax.psum_scatter(stacked(grads_gate), ("dp", "row"), scatter_dimension=1, tiled=True),
-        lax.psum_scatter(stacked(grads_inner), ("dp", "row"), scatter_dimension=1, tiled=True),
-        lax.psum_scatter(stacked(grads_pair), ("dp", "row"), scatter_dimension=1, tiled=True),
-        lax.psum_scatter(stacked(grads_step), ("dp", "row"), scatter_dimension=1, tiled=True),
-        lax.psum_scatter(stacked(grads_out), ("dp", "row"), scatter_dimension=1, tiled=True),
-    )
-    smalls = lax.psum(
-        (
-            column(0),
-            column(1),
-            column(2),
-            column(3),
-            column(4),
-            column(5),
-            column(6),
-            column(7),
-            column(8),
-        ),
-        ("dp", "row"),
-    )
+        low_grads = jnp.concatenate([d_gate16, d_inner16, d_pair16, d_step16], axis=1)
+        grad_in = lax.dot_general(normed_all, low_grads, dims_w, preferred_element_type=jnp.float32)
+        layer_grads = jnp.concatenate(
+            [grad_out.astype(jnp.bfloat16), grad_in.astype(jnp.bfloat16)], axis=1
+        )
+        layer_grads = jnp.pad(layer_grads, ((0, 0), (0, -layer_grads.shape[1] % 128)))
+        big_grads[layer_at] = lax.psum_scatter(
+            layer_grads, ("dp", "row"), scatter_dimension=0, tiled=True
+        ).astype(jnp.float32)
+        turned = backward_turn(
+            partial_in, resid_grad, resid, row_scale, norm_gain[layer_at], layer_at > 0
+        )
+        resid_grad, gain_in = turned[0], turned[1][0]
+        if layer_at > 0:
+            cot_all = turned[2]
+        small_terms[layer_at] = (
+            gain_in,
+            gain_y,
+            kernel_grad[:, :inner_cols],
+            bias_grad[:inner_cols],
+            kernel_grad[:, inner_cols:],
+            bias_grad[inner_cols:],
+            g_step_bias,
+            g_decay,
+            g_skip,
+        )
+
+    model_cols = output_weight.shape[1]
+    sizes = (model_cols, inner_cols, inner_cols, share_cols, head_count)
+    summed, at = [], 0
+    for size in sizes:
+        summed.append(jnp.stack([big[:, at : at + size] for big in big_grads], axis=0))
+        at += size
+    shapes = [part.shape for terms in small_terms for part in terms]
+    unpacked = unpacked_small(
+        small_total(packed_small([part for terms in small_terms for part in terms])), shapes
+    )
+    count = len(small_terms[0])
+    smalls = [
+        jnp.stack([unpacked[layer_at * count + slot] for layer_at in range(LAYERS)], axis=0)
+        for slot in range(count)
+    ]
     return (
         layer_output,
         resid_grad,
         smalls[0],
-        summed[0],
         summed[1],
         summed[2],
         summed[3],
-        smalls[2],
+        summed[4],
+        jnp.swapaxes(smalls[2], 1, 2),
         smalls[3],
-        smalls[4],
+        jnp.swapaxes(smalls[4], 1, 2),
         smalls[5],
         smalls[6],
         smalls[7],
         smalls[8],
         smalls[1],
-        jnp.transpose(summed[4], (0, 2, 1)),
+        jnp.transpose(summed[0], (0, 2, 1)),
     )
 
 

time: 732 us -> 535 us (0.73)
  blocking collectives: 237 us -> 0 us
  waiting for transfers between devices: 267 us -> 91.9 us
  Pallas kernels: 0 us -> 124 us
  local copies, waits for them, and re-layouts: 47.9 us -> 87.3 us
  starting transfers between devices: 9.14 us -> 37.8 us
  other arithmetic: 61.8 us -> 85.4 us
    reduce_scatter x7 -> x0, waiting for transfers between devices: 249 us -> none  [the longest x1 55.5 us: local(): lax.psum_scatter(stacked(grads_gate), ('dp', 'row'), scatter_dimension=1,...]
    all_gather x14 -> x0, blocking collectives: 130 us -> none  [the longest x6 37.5 us: carried_in(): gathered = jax.tree.map(lambda a: lax.all_gather(a, axis), part)]
    pallas_call x0 -> x9, Pallas kernels: none -> 124 us  [the longest x2 44.8 us: backward_turn(): pl.pallas_call(functools.partial(backward_turn_kernel, n, spread), out_sh...]
    psum x9 -> x0, blocking collectives: 106 us -> none  [the longest x8 80.5 us: row_total(): return lax.psum(values, 'col')]
    unnamed x19 -> x9, waiting for transfers between devices: 11.3 us -> 49.8 us
    ppermute x0 -> x17, waiting for transfers between devices: none -> 33.4 us  [the longest x10 30.3 us: whole_over_row(): other = lax.ppermute(block, 'row', [(0, 1), (1, 0)])]
    ppermute x0 -> x17, starting transfers between devices: none -> 25.6 us  [the longest x10 10.3 us: whole_over_row(): other = lax.ppermute(block, 'row', [(0, 1), (1, 0)])]
    concatenate x0 -> x12, other arithmetic: none -> 21.9 us  [the longest x10 17.8 us: whole_over_row(): trio = jnp.concatenate([block, other, block], axis=axis)]
  transfers between devices with their start and end apart: 21 -> 26, of which waited for: 11 -> 9; matrix products, arithmetic and copies ran while one was open for 14% -> 30% of each run, Pallas kernels for 0% -> 8%
where the time goes in v1:
time: 535 us; the launch traced here: 527 us
  Pallas kernels  124 us (23%)
  waiting for transfers between devices  91.9 us (17%)
  local copies, waits for them, and re-layouts  87.3 us (16%)
  other arithmetic  85.4 us (16%)
  matrix products  82.4 us (15%)
  starting transfers between devices  37.8 us (7%)
  between operations  17.7 us (3%)
    unnamed x9, waiting for transfers between devices  49.8 us
    pallas_call x2, Pallas kernels, backward_turn(): pl.pallas_call(functools.partial(backward_turn_kernel, n, spread), out_sh...  44.8 us
    ppermute x10, waiting for transfers between devices, whole_over_row(): other = lax.ppermute(block, 'row', [(0, 1), (1, 0)])  30.3 us
    unnamed x304, local copies, waits for them, and re-layouts  28.5 us
    pallas_call x4, Pallas kernels, row_total(): pl.pallas_call(functools.partial(row_sum_kernel, n), out_shape=jax.ShapeD...  28.2 us
    pallas_call x1, Pallas kernels, forward_turn(): pl.pallas_call(functools.partial(forward_turn_kernel, n), out_shape=[jax....  27 us
    dot_general x6, matrix products, mixer_parts(): intra_part = jnp.einsum('chij,cjhp->cihp', weights, xs_c, precision=HIGHEST)  23.5 us
    concatenate x10, other arithmetic, whole_over_row(): trio = jnp.concatenate([block, other, block], axis=axis)  17.8 us
  transfers between devices with their start and end apart: 26, of which 9 were waited for; matrix products, arithmetic and copies ran while one was open for 30% of the time, Pallas kernels for 8%

profile of v1, /device:TPU:0, one launch (start us, length us, event | category | flops | bytes accessed | tf_op | source)
XLA Modules:
  0.0 526.5 jit_solution(17607148013343440924)
XLA Ops:
  7.3 5.1 collective-permute-start.14
  20.4 16.2 %entry_gather.1 = (bf16[256,1024]{1,0:T(8,128)(2,1)}, f32[4,1,256]{2,1,0:T(1,128)}) custom-call(bf16[256,256]{1,0:T(8,128)(2,1)} %tok_ref.1, f32[1,256]{1,0:T(1,128)} %get-tuple-element.378.gain_ref), custom_call_target="tpu_custom_call" | custom-call | tf_op jit(solution)/shard_map/entry_gather/pallas_call | solution.py:260
  43.2 2.2 slice_bitcast_fusion.1
  46.7 2.0 compare_convert_fusion.3
  70.7 30.3 %collective-permute-done.8 = bf16[512,256]{1,0:T(8,128)(2,1)S(1)} collective-permute-done((bf16[512,256]{1,0:T(8,128)(2,1)S(1)}, bf16[512,256]{1,0:T(8,128)(2,1)S(1)}, u32[]{:S(2)}, u32[]{:S(2)}) %collective-permute-start.8) | collective-permute-done | bytes 262176 | tf_op jit(solution)/shard_map/ppermute | solution.py:316
  103.9 2.2 fusion.58
  106.7 2.6 collective-permute-start.2
  110.9 3.9 fusion.56
  116.3 3.5 fusion.52
  119.8 2.3 collective-permute-done.2
  126.4 4.6 collective-permute-start.4
  131.0 3.1 fusion.50
  135.3 3.4 bitcast_add_fusion.3
  138.7 2.0 copy.318
  140.7 3.5 multiply_reduce_fusion.15
  144.3 6.7 %row_total.4 = f32[1,256]{1,0:T(1,128)} custom-call(f32[1,256]{1,0:T(1,128)} %bitcast.657), custom_call_target="tpu_custom_call" | custom-call | tf_op jit(solution)/shard_map/row_total/pallas_call | solution.py:94
  151.7 2.5 fusion.292.part_ref
  154.2 27.0 %forward_turn.1 = (f32[256,256]{1,0:T(8,128)}, f32[256,1]{1,0:T(8,128)}, bf16[256,1024]{1,0:T(8,128)(2,1)}) custom-call(f32[256,1024]{1,0:T(8,128)} %fusion.292.part_ref, f32[256,256]{1,0:T(8,128)} %convert_element_type.139.resid_ref, f32[1,256]{1,0:T(1,128)} %get-tuple-element.377.gain_ref), custom_call_target="tpu_custom_call" | custom-call | tf_op jit(solution)/shard_map/forward_turn/pallas_call | solution.py:206
  186.9 1.7 fusion.325
  188.6 6.4 %collective-permute-start.9 = (f32[3,768]{1,0:T(4,128)S(1)}, f32[3,768]{1,0:T(4,128)}, u32[]{:S(2)}, u32[]{:S(2)}) collective-permute-start(f32[3,768]{1,0:T(4,128)S(1)} %fusion.226), channel_id=1, source_target_pairs={{0,4},{1,5},{2,6},{3,7},{8,12},{9,13},{10,14},{11,15},{16,20},{17,... | collective-permute-start | bytes 27656 | tf_op jit(solution)/shard_map/ppermute | solution.py:22
  196.7 2.1 copy.326
  200.2 2.5 divide_multiply_fusion
  205.7 1.7 convolution_add_fusion.4
  207.4 1.8 collective-permute-start.11
  213.8 3.4 bitcast_add_fusion.2
  219.3 3.3 multiply_reduce_fusion.14
  222.6 7.2 %row_total.5 = f32[1,256]{1,0:T(1,128)} custom-call(f32[1,256]{1,0:T(1,128)} %bitcast.658), custom_call_target="tpu_custom_call" | custom-call | tf_op jit(solution)/shard_map/row_total/pallas_call | solution.py:94
  230.5 3.4 multiply_reduce_fusion.7
  233.9 6.7 %row_total.6 = f32[1,256]{1,0:T(1,128)} custom-call(f32[1,256]{1,0:T(1,128)} %bitcast.635), custom_call_target="tpu_custom_call" | custom-call | tf_op jit(solution)/shard_map/row_total/pallas_call | solution.py:94
  241.2 3.4 multiply_reduce_fusion.6
  244.6 2.0 copy.324
  246.7 1.9 multiply_reduce_fusion.12
  248.5 5.4 %fusion.41 = (f32[8,256]{1,0:T(8,128)}, f32[8,256]{1,0:T(8,128)}, f32[8,256]{1,0:T(8,128)}, f32[256,256]{1,0:T(8,128)S(1)}) fusion(f32[8,256]{1,0:T(8,128)S(1)} %copy-done.105, f32[256,256]{1,0:T(8,128)} %copy-done.64, f32[8,256]{1,0:T(8,128)S(1)} %copy-done.110, f32[256,256]{1,0:T(8,128)} %fusion.187, f32[8,64,256]{2,1,0:T(8,128)} %bitcast.588, ...), kind=kOutput, calls=%fused_computation.81 | convolution fusion | flops 410445824 | bytes 1875968 | tf_op jit(solution)/shard_map/transpose(jvp(chij,cjhp->cihp))/dot_general | solution.py:383
  259.5 2.1 copy.327
  261.5 1.7 fusion.38
  264.8 1.7 fusion.37
  267.5 1.7 multiply_reduce_fusion.5
  269.3 4.2 bitcast_add_fusion.1
  273.5 2.1 copy.329
  278.6 2.5 reduce-window.50
  281.3 7.0 %reduce-scatter.16.cloned.1.call-done = f32[64,256]{1,0:T(8,128)} async-done(((f32[256,256]{1,0:T(8,128)}), f32[64,256]{1,0:T(8,128)}) %reduce-scatter.16.cloned.1.call-update) | async-done | bytes 65552
  289.2 2.9 fusion.102
  294.8 2.8 collective-permute-done.18
  302.7 27.3 %backward_turn.1 = (f32[256,256]{1,0:T(8,128)}, f32[1,256]{1,0:T(1,128)}, bf16[256,1024]{1,0:T(8,128)(2,1)}) custom-call(f32[256,1024]{1,0:T(8,128)} %convolution_add_fusion.1.part_ref, f32[256,256]{1,0:T(8,128)} %get-tuple-element.328.grad_ref, f32[256,256]{1,0:T(8,128)} %get-tuple-element.133.resid_ref, f32[256,1]{1,0:T(8,128)} %get-tuple-element.144.scale_ref, ...), custom_call_target="tpu_custom_call" | custom-call | tf_op jit(solution)/shard_map/backward_turn/pallas_call | solution.py:230
  330.0 3.3 multiply_reduce_fusion.9
  333.4 7.6 %row_total.7 = f32[1,256]{1,0:T(1,128)} custom-call(f32[1,256]{1,0:T(1,128)} %bitcast.641), custom_call_target="tpu_custom_call" | custom-call | tf_op jit(solution)/shard_map/row_total/pallas_call | solution.py:94
  341.6 3.2 multiply_reduce_fusion.8
  346.1 5.2 fusion.43
  357.0 2.1 copy.336
  364.6 2.7 fusion.293
  367.4 2.6 convolution_convert_fusion.2
  372.5 2.0 pad_maximum_fusion.1
  374.6 5.5 %copy.365 = bf16[1024,1608]{1,0:T(8,128)(2,1)} copy(bf16[1024,1608]{0,1:T(8,128)(2,1)} %pad_maximum_fusion.1) | data formatting | bytes 6586368
  380.0 3.9 pad.31.clone
  387.1 1.9 slice.696
  398.3 2.0 bitcast_add_fusion
  402.2 2.5 reduce-window.56
  409.4 3.7 collective-permute-done.20
  415.6 2.1 pad_maximum_fusion
  417.7 4.4 copy.364
  422.1 2.0 pad.30.clone
  429.3 17.6 %backward_end.1 = (f32[256,256]{1,0:T(8,128)}, f32[1,256]{1,0:T(1,128)}) custom-call(f32[256,1024]{1,0:T(8,128)} %convolution_add_fusion.part_ref, f32[256,256]{1,0:T(8,128)} %get-tuple-element.148.grad_ref, f32[256,256]{1,0:T(8,128)} %convert_element_type.139.resid_ref, f32[256,1]{1,0:T(8,128)} %copy.341.scale_ref, f32[1,256]{1,0:T(1,128)} %get-tuple-element.378.gain_ref), custom_call_target="tpu_custom_call" | custom-call | tf_op jit(solution)/shard_map/backward_end/pallas_call | solution.py:230
  448.3 7.9 %small_total.1 = f32[64,128]{1,0:T(8,128)} custom-call(f32[64,128]{1,0:T(8,128)} %pad_bitcast_fusion.value_ref), custom_call_target="tpu_custom_call" | custom-call | tf_op jit(solution)/shard_map/small_total/pallas_call | solution.py:298
  470.8 42.7 %reduce-scatter.20.cloned.1.call-done = bf16[128,1664]{1,0:T(8,128)(2,1)} async-done(((bf16[1024,1664]{1,0:T(8,128)(2,1)}), bf16[128,1664]{1,0:T(8,128)(2,1)}) %reduce-scatter.20.cloned.1.call-update) | async-done | bytes 426000
  (564 shorter events, 152.1 us)
Async XLA Ops:
  7.2 30.6 %copy-start.49 = (bf16[2,512,512]{2,1,0:T(8,128)(2,1)S(1)}, bf16[2,512,512]{2,1,0:T(8,128)(2,1)}, u32[]{:S(2)}) copy-start(bf16[2,512,512]{2,1,0:T(8,128)(2,1)} %param.23) | copy-start | bytes 3145732
  7.3 281.0 %reduce-scatter.16.cloned.1.call-start = ((), (), s32[]{:S(2)}) async-start(), calls=%async_computation.6 | async-start | bytes 327680
  7.3 49.3 %collective-permute-start.14 = (bf16[256,256]{1,0:T(8,128)(2,1)}, bf16[256,256]{1,0:T(8,128)(2,1)}, u32[]{:S(2)}, u32[]{:S(2)}) collective-permute-start(bf16[256,256]{1,0:T(8,128)(2,1)} %param.20), channel_id=1, source_target_pairs={{0,3},{1,0},{2,1},{3,2},{4,7},{5,4},{6,5},{7,6},{8,11},{9,8},{10,9... | collective-permute-start | bytes 393224 | tf_op jit(solution)/shard_map/ppermute | solution.py:327
  12.4 47.3 %collective-permute-start.15 = (bf16[256,256]{1,0:T(8,128)(2,1)}, bf16[256,256]{1,0:T(8,128)(2,1)}, u32[]{:S(2)}, u32[]{:S(2)}) collective-permute-start(bf16[256,256]{1,0:T(8,128)(2,1)} %param.20), channel_id=1, source_target_pairs={{0,2},{1,3},{2,0},{3,1},{4,6},{5,7},{6,4},{7,5},{8,10},{9,11},{10,... | collective-permute-start | bytes 393224 | tf_op jit(solution)/shard_map/ppermute | solution.py:327
  12.4 49.4 %collective-permute-start.16 = (bf16[256,256]{1,0:T(8,128)(2,1)}, bf16[256,256]{1,0:T(8,128)(2,1)}, u32[]{:S(2)}, u32[]{:S(2)}) collective-permute-start(bf16[256,256]{1,0:T(8,128)(2,1)} %param.20), channel_id=1, source_target_pairs={{0,1},{1,2},{2,3},{3,0},{4,5},{5,6},{6,7},{7,4},{8,9},{9,10},{10,1... | collective-permute-start | bytes 393224 | tf_op jit(solution)/shard_map/ppermute | solution.py:327
  14.7 92.0 %collective-permute-start.6 = (bf16[512,512]{1,0:T(8,128)(2,1)S(1)}, bf16[512,512]{1,0:T(8,128)(2,1)}, u32[]{:S(2)}, u32[]{:S(2)}) collective-permute-start(bf16[512,512]{1,0:T(8,128)(2,1)S(1)} %get-tuple-element.319), channel_id=1, source_target_pairs={{0,4},{4,0},{1,5},{5,1},{2,6},{6,2},{3,7},{7,3},{8,12},{12,8},{9,1... | collective-permute-start | bytes 1572872 | tf_op jit(solution)/shard_map/ppermute | solution.py:316
  16.2 33.7 %collective-permute-start.3 = (bf16[512,8]{0,1:T(8,128)(2,1)S(1)}, bf16[512,8]{0,1:T(8,128)(2,1)S(1)}, u32[]{:S(2)}, u32[]{:S(2)}) collective-permute-start(bf16[512,8]{0,1:T(8,128)(2,1)S(1)} %get-tuple-element.349), channel_id=1, source_target_pairs={{0,4},{4,0},{1,5},{5,1},{2,6},{6,2},{3,7},{7,3},{8,12},{12,8},{9,1... | collective-permute-start | bytes 24584 | tf_op jit(solution)/shard_map/ppermute | solution.py:316
  18.3 20.4 %copy-start.99 = (f32[2,256,4]{1,2,0:T(4,128)S(1)}, f32[2,256,4]{1,2,0:T(4,128)}, u32[]{:S(2)}) copy-start(f32[2,256,4]{1,2,0:T(4,128)} %param.28) | copy-start | bytes 24580
  18.3 20.4 %copy-start.87 = (f32[2,512,4]{1,2,0:T(4,128)S(1)}, f32[2,512,4]{1,2,0:T(4,128)}, u32[]{:S(2)}) copy-start(f32[2,512,4]{1,2,0:T(4,128)} %param.26) | copy-start | bytes 49156
  18.3 21.9 %copy-start.133 = (f32[2,256]{1,0:T(2,128)S(1)}, f32[2,256]{1,0:T(2,128)}, u32[]{:S(2)}) copy-start(f32[2,256]{1,0:T(2,128)} %param.29) | copy-start | bytes 6148
  18.3 21.8 %copy-start.124 = (f32[2,512]{1,0:T(2,128)S(1)}, f32[2,512]{1,0:T(2,128)}, u32[]{:S(2)}) copy-start(f32[2,512]{1,0:T(2,128)} %param.27) | copy-start | bytes 12292
  18.3 21.9 %copy-start.135 = (f32[2,8]{1,0:T(2,128)S(1)}, f32[2,8]{1,0:T(2,128)}, u32[]{:S(2)}) copy-start(f32[2,8]{1,0:T(2,128)} %param.30) | copy-start | bytes 196
  18.4 22.4 %copy-start.122 = (f32[2,8]{1,0:T(2,128)S(1)}, f32[2,8]{1,0:T(2,128)}, u32[]{:S(2)}) copy-start(f32[2,8]{1,0:T(2,128)} %param.31) | copy-start | bytes 196
  18.4 24.2 %copy-start.136 = (f32[2,8]{1,0:T(2,128)S(1)}, f32[2,8]{1,0:T(2,128)}, u32[]{:S(2)}) copy-start(f32[2,8]{1,0:T(2,128)} %param.32) | copy-start | bytes 196
  37.8 102.9 %copy-start.93 = (f32[256]{0:T(256)}, f32[256]{0:T(256)S(1)}, u32[]{:S(2)}) copy-start(f32[256]{0:T(256)S(1)} %add_rsqrt_fusion.2) | copy-start | bytes 3076
  38.7 16.1 %copy-start.50 = (bf16[512,256]{1,0:T(8,128)(2,1)S(1)}, bf16[512,256]{1,0:T(8,128)(2,1)}, u32[]{:S(2)}) copy-start(bf16[512,256]{1,0:T(8,128)(2,1)} %get-tuple-element.327) | copy-start | bytes 786436
  45.4 19.5 %copy-start.56 = (bf16[256,256]{1,0:T(8,128)(2,1)S(1)}, bf16[256,256]{1,0:T(8,128)(2,1)}, u32[]{:S(2)}) copy-start(bf16[256,256]{1,0:T(8,128)(2,1)} %param.20) | copy-start | bytes 393220
  45.4 106.2 %copy-start.67 = (f32[1,512]{1,0:T(1,128)}, f32[1,512]{1,0:T(1,128)S(1)}, u32[]{:S(2)}) copy-start(f32[1,512]{1,0:T(1,128)S(1)} %get-tuple-element.365) | copy-start | bytes 6148
  48.6 18.5 %copy-start.74 = (f32[256]{0:T(256)}, f32[256]{0:T(256)S(1)}, u32[]{:S(2)}) copy-start(f32[256]{0:T(256)S(1)} %get-tuple-element.368) | copy-start | bytes 3076
  48.6 73.5 %copy-start.76 = (f32[256]{0:T(256)}, f32[256]{0:T(256)S(1)}, u32[]{:S(2)}) copy-start(f32[256]{0:T(256)S(1)} %get-tuple-element.370) | copy-start | bytes 3076
  48.6 73.5 %copy-start.78 = (f32[256]{0:T(256)}, f32[256]{0:T(256)S(1)}, u32[]{:S(2)}) copy-start(f32[256]{0:T(256)S(1)} %get-tuple-element.371) | copy-start | bytes 3076
  48.6 73.5 %copy-start.80 = (f32[256]{0:T(256)}, f32[256]{0:T(256)S(1)}, u32[]{:S(2)}) copy-start(f32[256]{0:T(256)S(1)} %get-tuple-element.372) | copy-start | bytes 3076
  50.0 4.9 collective-permute-start.10
  54.3 16.0 %copy-start.88 = (f32[8]{0:T(128)}, f32[8]{0:T(128)S(1)}, u32[]{:S(2)}) copy-start(f32[8]{0:T(128)S(1)} %slice_reduce_fusion.5) | copy-start | bytes 100
  54.9 13.8 %collective-permute-start.1 = (bf16[512,256]{1,0:T(8,128)(2,1)S(1)}, bf16[512,256]{1,0:T(8,128)(2,1)}, u32[]{:S(2)}, u32[]{:S(2)}) collective-permute-start(bf16[512,256]{1,0:T(8,128)(2,1)S(1)} %copy-done.50), channel_id=1, source_target_pairs={{0,4},{4,0},{1,5},{5,1},{2,6},{6,2},{3,7},{7,3},{8,12},{12,8},{9,1... | collective-permute-start | bytes 786440 | tf_op jit(solution)/shard_map/ppermute | solution.py:316
  56.6 45.8 %collective-permute-start = (bf16[512,512]{1,0:T(8,128)(2,1)S(1)}, bf16[512,512]{1,0:T(8,128)(2,1)S(1)}, u32[]{:S(2)}, u32[]{:S(2)}) collective-permute-start(bf16[512,512]{1,0:T(8,128)(2,1)S(1)} %get-tuple-element.317), channel_id=1, source_target_pairs={{0,4},{4,0},{1,5},{5,1},{2,6},{6,2},{3,7},{7,3},{8,12},{12,8},{9,1... | collective-permute-start | bytes 1572872 | tf_op jit(solution)/shard_map/ppermute | solution.py:316
  59.7 51.2 %collective-permute-start.5 = (bf16[512,512]{1,0:T(8,128)(2,1)}, bf16[512,512]{1,0:T(8,128)(2,1)S(1)}, u32[]{:S(2)}, u32[]{:S(2)}) collective-permute-start(bf16[512,512]{1,0:T(8,128)(2,1)} %get-tuple-element.315), channel_id=1, source_target_pairs={{0,4},{4,0},{1,5},{5,1},{2,6},{6,2},{3,7},{7,3},{8,12},{12,8},{9,1... | collective-permute-start | bytes 1572872 | tf_op jit(solution)/shard_map/ppermute | solution.py:316
  61.8 53.0 %collective-permute-start.13 = (bf16[512,512]{1,0:T(8,128)(2,1)S(1)}, bf16[512,512]{1,0:T(8,128)(2,1)S(1)}, u32[]{:S(2)}, u32[]{:S(2)}) collective-permute-start(bf16[512,512]{1,0:T(8,128)(2,1)S(1)} %get-tuple-element.318), channel_id=1, source_target_pairs={{0,4},{4,0},{1,5},{5,1},{2,6},{6,2},{3,7},{7,3},{8,12},{12,8},{9,1... | collective-permute-start | bytes 1572872 | tf_op jit(solution)/shard_map/ppermute | solution.py:316
  68.7 32.2 %collective-permute-start.8 = (bf16[512,256]{1,0:T(8,128)(2,1)S(1)}, bf16[512,256]{1,0:T(8,128)(2,1)S(1)}, u32[]{:S(2)}, u32[]{:S(2)}) collective-permute-start(bf16[512,256]{1,0:T(8,128)(2,1)S(1)} %get-tuple-element.326), channel_id=1, source_target_pairs={{0,4},{4,0},{1,5},{5,1},{2,6},{6,2},{3,7},{7,3},{8,12},{12,8},{9,1... | collective-permute-start | bytes 786440 | tf_op jit(solution)/shard_map/ppermute | solution.py:316
  70.3 35.9 %copy-start.48 = (bf16[1536,256]{1,0:T(8,128)(2,1)}, bf16[1536,256]{1,0:T(8,128)(2,1)S(1)}, u32[]{:S(2)}) copy-start(bf16[1536,256]{1,0:T(8,128)(2,1)S(1)} %pad_maximum_fusion.4) | copy-start | bytes 2359300
  100.9 15.4 %collective-permute-start.7 = (bf16[512,512]{1,0:T(8,128)(2,1)}, bf16[512,512]{1,0:T(8,128)(2,1)S(1)}, u32[]{:S(2)}, u32[]{:S(2)}) collective-permute-start(bf16[512,512]{1,0:T(8,128)(2,1)} %get-tuple-element.316), channel_id=1, source_target_pairs={{0,4},{4,0},{1,5},{5,1},{2,6},{6,2},{3,7},{7,3},{8,12},{12,8},{9,1... | collective-permute-start | bytes 1572872 | tf_op jit(solution)/shard_map/ppermute | solution.py:316
  102.4 28.6 %collective-permute-start.12 = (bf16[512,512]{1,0:T(8,128)(2,1)}, bf16[512,512]{1,0:T(8,128)(2,1)}, u32[]{:S(2)}, u32[]{:S(2)}) collective-permute-start(bf16[512,512]{1,0:T(8,128)(2,1)} %get-tuple-element.314), channel_id=1, source_target_pairs={{0,4},{4,0},{1,5},{5,1},{2,6},{6,2},{3,7},{7,3},{8,12},{12,8},{9,1... | collective-permute-start | bytes 1572872 | tf_op jit(solution)/shard_map/ppermute | solution.py:316
  106.7 15.4 %collective-permute-start.2 = (f32[3,768]{1,0:T(4,128)S(1)}, f32[3,768]{1,0:T(4,128)S(1)}, u32[]{:S(2)}, u32[]{:S(2)}) collective-permute-start(f32[3,768]{1,0:T(4,128)S(1)} %fusion.227), channel_id=1, source_target_pairs={{0,4},{1,5},{2,6},{3,7},{8,12},{9,13},{10,14},{11,15},{16,20},{17,... | collective-permute-start | bytes 27656 | tf_op jit(solution)/shard_map/ppermute | solution.py:22
  110.9 40.8 %copy-start.6 = (bf16[512,1024]{1,0:T(8,128)(2,1)}, bf16[512,1024]{1,0:T(8,128)(2,1)S(1)}, u32[]{:S(2)}) copy-start(bf16[512,1024]{1,0:T(8,128)(2,1)S(1)} %fusion.54) | copy-start | bytes 3145732
  122.1 263.9 %copy-start = (f32[259,768]{1,0:T(8,128)}, f32[259,768]{1,0:T(8,128)S(1)}, u32[]{:S(2)}) copy-start(f32[259,768]{1,0:T(8,128)S(1)} %maximum_maximum_fusion) | copy-start | bytes 2386948
  126.4 8.3 %collective-permute-start.4 = (f32[8,64,128]{2,1,0:T(8,128)S(1)}, f32[8,64,128]{2,1,0:T(8,128)S(1)}, u32[]{:S(2)}, u32[]{:S(2)}) collective-permute-start(f32[8,64,128]{2,1,0:T(8,128)S(1)} %convolution_add_fusion.5), channel_id=1, source_target_pairs={{0,4},{1,5},{2,6},{3,7},{8,12},{9,13},{10,14},{11,15},{16,20},{17,... | collective-permute-start | bytes 786440 | tf_op jit(solution)/shard_map/ppermute | solution.py:29
  144.3 36.9 %copy-start.130 = (f32[8]{0:T(128)S(1)}, f32[8]{0:T(128)}, u32[]{:S(2)}) copy-start(f32[8]{0:T(128)} %get-tuple-element.383) | copy-start | bytes 100
  151.7 30.9 %copy-start.71 = (f32[1,256]{1,0:T(1,128)}, f32[1,256]{1,0:T(1,128)S(1)}, u32[]{:S(2)}) copy-start(f32[1,256]{1,0:T(1,128)S(1)} %add_rsqrt_fusion.1) | copy-start | bytes 3076
  151.7 30.9 %copy-start.116 = (f32[8]{0:T(128)S(1)}, f32[8]{0:T(128)}, u32[]{:S(2)}) copy-start(f32[8]{0:T(128)} %get-tuple-element.385) | copy-start | bytes 100
  188.6 10.2 %collective-permute-start.9 = (f32[3,768]{1,0:T(4,128)S(1)}, f32[3,768]{1,0:T(4,128)}, u32[]{:S(2)}, u32[]{:S(2)}) collective-permute-start(f32[3,768]{1,0:T(4,128)S(1)} %fusion.226), channel_id=1, source_target_pairs={{0,4},{1,5},{2,6},{3,7},{8,12},{9,13},{10,14},{11,15},{16,20},{17,... | collective-permute-start | bytes 27656 | tf_op jit(solution)/shard_map/ppermute | solution.py:22
  207.4 5.6 %collective-permute-start.11 = (f32[8,64,128]{2,1,0:T(8,128)S(1)}, f32[8,64,128]{2,1,0:T(8,128)S(1)}, u32[]{:S(2)}, u32[]{:S(2)}) collective-permute-start(f32[8,64,128]{2,1,0:T(8,128)S(1)} %convolution_add_fusion.4), channel_id=1, source_target_pairs={{0,4},{1,5},{2,6},{3,7},{8,12},{9,13},{10,14},{11,15},{16,20},{17,... | collective-permute-start | bytes 786440 | tf_op jit(solution)/shard_map/ppermute | solution.py:29
  222.6 18.7 %copy-start.5 = (f32[256,768]{1,0:T(8,128)S(1)}, f32[256,768]{1,0:T(8,128)}, u32[]{:S(2)}) copy-start(f32[256,768]{1,0:T(8,128)} %copy-done.3) | copy-start | bytes 2359300
  256.2 8.6 %collective-permute-start.17 = (f32[8,64,128]{2,1,0:T(8,128)}, f32[8,64,128]{2,1,0:T(8,128)}, u32[]{:S(2)}, u32[]{:S(2)}) collective-permute-start(f32[8,64,128]{2,1,0:T(8,128)} %fusion.151), channel_id=1, source_target_pairs={{4,0},{5,1},{6,2},{7,3},{12,8},{13,9},{14,10},{15,11},{20,16},{21,... | collective-permute-start | bytes 786440 | tf_op jit(solution)/shard_map/ppermute | solution.py:29
  267.3 137.6 %reduce-scatter.18.cloned.1.call-start = ((), (), s32[]{:S(2)}) async-start(), calls=%async_computation.7 | async-start | bytes 327680
  269.3 19.9 %slice-start.2 = ((f32[259,768]{1,0:T(8,128)}), f32[259,512]{1,0:T(8,128)S(1)}, s32[]{:S(2)}) async-start(f32[259,768]{1,0:T(8,128)} %copy-done.1), calls=%async_computation.12 | async-start | bytes 1081344 | tf_op jit(solution)/shard_map/slice | solution.py:673
  292.1 5.6 %collective-permute-start.18 = (f32[3,576]{1,0:T(4,128)S(1)}, f32[3,576]{1,0:T(4,128)S(1)}, u32[]{:S(2)}, u32[]{:S(2)}) collective-permute-start(f32[3,576]{1,0:T(4,128)S(1)} %slice.682), channel_id=1, source_target_pairs={{4,0},{5,1},{6,2},{7,3},{12,8},{13,9},{14,10},{15,11},{20,16},{21,... | collective-permute-start | bytes 20744 | tf_op jit(solution)/shard_map/ppermute | solution.py:22
  301.3 28.7 %copy-start.10 = (f32[256,512]{1,0:T(8,128)S(1)}, f32[256,512]{1,0:T(8,128)}, u32[]{:S(2)}) copy-start(f32[256,512]{1,0:T(8,128)} %get-tuple-element.307) | copy-start | bytes 1572868
  301.4 28.7 %copy-start.68 = (f32[1,512]{1,0:T(1,128)S(1)}, f32[1,512]{1,0:T(1,128)}, u32[]{:S(2)}) copy-start(f32[1,512]{1,0:T(1,128)} %copy-done.67) | copy-start | bytes 6148
  301.4 28.7 %copy-start.72 = (f32[1,256]{1,0:T(1,128)S(1)}, f32[1,256]{1,0:T(1,128)}, u32[]{:S(2)}) copy-start(f32[1,256]{1,0:T(1,128)} %copy-done.71) | copy-start | bytes 3076
  353.6 8.6 %collective-permute-start.19 = (f32[8,64,128]{2,1,0:T(8,128)}, f32[8,64,128]{2,1,0:T(8,128)}, u32[]{:S(2)}, u32[]{:S(2)}) collective-permute-start(f32[8,64,128]{2,1,0:T(8,128)} %fusion.149), channel_id=1, source_target_pairs={{4,0},{5,1},{6,2},{7,3},{12,8},{13,9},{14,10},{15,11},{20,16},{21,... | collective-permute-start | bytes 786440 | tf_op jit(solution)/shard_map/ppermute | solution.py:29
  364.5 103.2 %reduce-scatter.14.cloned.1.call-start = ((), (), s32[]{:S(2)}) async-start(), calls=%async_computation.5 | async-start | bytes 1310720 | tf_op jit(solution)/shard_map/reduce_scatter | solution.py:576
  367.3 102.0 %reduce-scatter.22.cloned.1.call-start = ((), (), s32[]{:S(2)}) async-start(), calls=%async_computation.9 | async-start | bytes 3833856
  384.1 129.4 %reduce-scatter.20.cloned.1.call-start = ((), (), s32[]{:S(2)}) async-start(), calls=%async_computation.8 | async-start | bytes 3833856
  407.5 5.6 %collective-permute-start.20 = (f32[3,576]{1,0:T(4,128)S(1)}, f32[3,576]{1,0:T(4,128)S(1)}, u32[]{:S(2)}, u32[]{:S(2)}) collective-permute-start(f32[3,576]{1,0:T(4,128)S(1)} %slice.698), channel_id=1, source_target_pairs={{4,0},{5,1},{6,2},{7,3},{12,8},{13,9},{14,10},{15,11},{20,16},{21,... | collective-permute-start | bytes 20744 | tf_op jit(solution)/shard_map/ppermute | solution.py:22
  427.9 19.0 %copy-start.96 = (f32[512]{0:T(512)S(1)}, f32[512]{0:T(512)}, u32[]{:S(2)}) copy-start(f32[512]{0:T(512)} %get-tuple-element.264) | copy-start | bytes 6148
  427.9 19.0 %copy-start.106 = (f32[512]{0:T(512)S(1)}, f32[512]{0:T(512)}, u32[]{:S(2)}) copy-start(f32[512]{0:T(512)} %slice.612) | copy-start | bytes 6148
  427.9 19.0 %copy-start.113 = (f32[512]{0:T(512)S(1)}, f32[512]{0:T(512)}, u32[]{:S(2)}) copy-start(f32[512]{0:T(512)} %get-tuple-element.266) | copy-start | bytes 6148
  427.9 19.0 %copy-start.121 = (f32[256]{0:T(256)S(1)}, f32[256]{0:T(256)}, u32[]{:S(2)}) copy-start(f32[256]{0:T(256)} %reshape.1365) | copy-start | bytes 3076
  427.9 19.0 %copy-start.126 = (f32[8]{0:T(128)S(1)}, f32[8]{0:T(128)}, u32[]{:S(2)}) copy-start(f32[8]{0:T(128)} %get-tuple-element.292) | copy-start | bytes 100
  427.9 19.0 %copy-start.127 = (f32[8]{0:T(128)S(1)}, f32[8]{0:T(128)}, u32[]{:S(2)}) copy-start(f32[8]{0:T(128)} %reduce_sum.505) | copy-start | bytes 100
  427.9 19.0 %copy-start.128 = (f32[8]{0:T(128)S(1)}, f32[8]{0:T(128)}, u32[]{:S(2)}) copy-start(f32[8]{0:T(128)} %reduce_sum.494) | copy-start | bytes 100
  427.9 19.0 %copy-start.134 = (f32[1,256]{1,0:T(1,128)S(1)}, f32[1,256]{1,0:T(1,128)}, u32[]{:S(2)}) copy-start(f32[1,256]{1,0:T(1,128)} %get-tuple-element.151) | copy-start | bytes 3076
  427.9 19.0 %copy-start.137 = (f32[64]{0:T(128)S(1)}, f32[64]{0:T(128)}, u32[]{:S(2)}) copy-start(f32[64]{0:T(128)} %slice.614) | copy-start | bytes 772
  427.9 39.8 %copy-start.51 = (f32[256,256]{1,0:T(8,128)S(1)}, f32[256,256]{1,0:T(8,128)}, u32[]{:S(2)}) copy-start(f32[256,256]{1,0:T(8,128)} %get-tuple-element.133.resid_ref) | copy-start | bytes 786436
  (108 other events, 652.7 us)
Sparse Core Ops, SparseCore 0:
  267.4 20.7 reduce-scatter.15
  364.6 20.4 reduce-scatter.17
  387.4 25.3 reduce-scatter.13
  416.5 46.1 reduce-scatter.21
  466.0 47.4 reduce-scatter.19
